TPU v7x, 256 devices: a whole 4x4x8 slice. The times are simulated.
256 devices in a mesh: ctx: 32 (over x, z), head: 8 (over y, core).
Axes of the slice: x: 4, y: 4, z: 8, core: 2. Of those that a mesh axis runs over, the one named last changes fastest.
Arguments:
- queries: float32 [32768, 768], P(('ctx', 'head')), may hold values from -280 to 280, as said below
- keys: float32 [32768, 768], P(('ctx', 'head')), may hold values from -7 to 7, as said below
- values: float32 [32768, 768], P(('ctx', 'head')), may hold values from -6 to 6
- grad_out: float32 [32768, 768], P(('ctx', 'head')), may hold values from -6 to 6
- neighbours: int32 [256, 2], replicated, may hold values from 0 to 255, as said below
- bias_index: int32 [256, 3], P('ctx'), may hold values from 0 to 15
- bias_table: float32 [16, 128, 128], replicated, may hold values from -6 to 6
- head_gain: float32 [16], P('head'), may hold values from 0.5 to 2
Outputs:
- attended: float32 [32768, 768], P(('ctx', 'head'))
- grad_queries: float32 [32768, 768], P(('ctx', 'head'))
- grad_keys: float32 [32768, 768], P(('ctx', 'head'))
- grad_values: float32 [32768, 768], P(('ctx', 'head'))
- grad_table: float32 [16, 128, 128], replicated
- grad_gain: float32 [16], P('head')
Inputs may be any that keep to these rules, and one draw needn't show every extreme that they name: `neighbours`: each entry names a block of another ctx shard (entry // 8 differs from the query block's b // 8). Among the rows of one ctx shard, at most 1 entries name blocks of one other shard, and at most 1 distinct blocks of it; both bounds are reached in every draw. `queries`: entries have magnitude at most 280. `keys`: entries have magnitude at most 7.
All inputs are finite; a program needn't handle non-finite values.
Results may differ from a plain program's by a relative error of at most 0.0003.
Values sent between devices are 32-bit elements; how exact they have to be, the bound alone decides.
A program may use at most 128 MiB of HBM per device.

v0:
```python
from functools import partial

import jax
import jax.numpy as jnp
from jax import lax
from jax.sharding import PartitionSpec as P

BLOCK = 128
NEI = 2


def attend(query_block, key_sets, value_sets, edge_bias, head_gain):
    head_count = head_gain.shape[0]
    block_rows = query_block.shape[0]
    set_blocks = key_sets.shape[0]
    query_heads = query_block.reshape(block_rows, head_count, -1)
    key_heads = key_sets.reshape(set_blocks, block_rows, head_count, -1)
    value_heads = value_sets.reshape(set_blocks * block_rows, head_count, -1)
    factor = query_heads.shape[2] ** (-0.5)
    scores = (
        jnp.einsum("ihd,mchd->himc", query_heads, key_heads, precision=lax.Precision.HIGHEST)
        * factor
    )
    scores = scores + head_gain[:, None, None, None] * jnp.transpose(edge_bias, (1, 0, 2))[None]
    scores = scores.reshape(head_count, block_rows, set_blocks * block_rows)
    maxima = lax.stop_gradient(jnp.max(scores, axis=-1, keepdims=True))
    weights = jnp.exp(scores - maxima)
    weights = weights / jnp.sum(weights, axis=-1, keepdims=True)
    result = jnp.einsum("hik,khd->ihd", weights, value_heads, precision=lax.Precision.HIGHEST)
    return result.reshape(block_rows, -1)


def request_slots(requests, blocks):
    owners = requests // blocks
    ordinal = jnp.arange(requests.shape[0], dtype=jnp.int32)
    earlier = ordinal[None, :] < ordinal[:, None]
    same_owner = owners[:, None] == owners[None, :]
    return jnp.sum((same_owner & earlier).astype(jnp.int32), axis=1)


def body(queries, keys, values, grad_out, neighbours, bias_index, bias_table, head_gain):
    shards = lax.axis_size("ctx")
    myself = lax.axis_index("ctx")
    head_query, head_key, head_value, head_grad = (
        lax.all_to_all(queries, "head", split_axis=1, concat_axis=0, tiled=True),
        lax.all_to_all(keys, "head", split_axis=1, concat_axis=0, tiled=True),
        lax.all_to_all(values, "head", split_axis=1, concat_axis=0, tiled=True),
        lax.all_to_all(grad_out, "head", split_axis=1, concat_axis=0, tiled=True),
    )
    length, columns = head_query.shape
    blocks = length // BLOCK
    requests = blocks * NEI
    capacity = (requests + shards - 2) // (shards - 1)
    all_requests = neighbours.reshape(shards, requests)
    slot_all = jax.vmap(partial(request_slots, blocks=blocks))(all_requests)
    owners = all_requests // blocks
    local_ids = all_requests % blocks
    from_me = owners == myself
    slot_ids = jnp.arange(capacity, dtype=jnp.int32)
    selected = from_me[:, None, :] & (slot_all[:, None, :] == slot_ids[None, :, None])
    send_ids = jnp.max(jnp.where(selected, local_ids[:, None, :], 0), axis=2).reshape(-1)
    filled = jnp.any(selected, axis=2).reshape(-1)
    packed = jnp.concatenate([head_key, head_value], axis=1).reshape(blocks, BLOCK, 2 * columns)
    outgoing = jnp.where(filled[:, None, None], packed[send_ids], 0.0)
    arrived = lax.all_to_all(outgoing, "ctx", split_axis=0, concat_axis=0, tiled=True)
    my_owners = lax.dynamic_index_in_dim(owners, myself, 0, keepdims=False)
    my_slots = lax.dynamic_index_in_dim(slot_all, myself, 0, keepdims=False)
    wanted = my_owners * capacity + my_slots
    remote = arrived[wanted].reshape(blocks, NEI, BLOCK, 2 * columns)
    gathered = jnp.concatenate([packed[:, None], remote], axis=1)
    edge_bias = bias_table[bias_index]
    forward = jax.vmap(attend, in_axes=(0, 0, 0, 0, None))
    result, pullback = jax.vjp(
        forward,
        head_query.reshape(blocks, BLOCK, columns),
        gathered[..., :columns],
        gathered[..., columns:],
        edge_bias,
        head_gain,
    )
    query_grad, key_grad, value_grad, bias_grad, gain_grad = pullback(
        head_grad.reshape(blocks, BLOCK, columns)
    )
    attended, grad_queries = (
        lax.all_to_all(
            result.reshape(length, columns), "head", split_axis=0, concat_axis=1, tiled=True
        ),
        lax.all_to_all(
            query_grad.reshape(length, columns), "head", split_axis=0, concat_axis=1, tiled=True
        ),
    )
    remote_grad = jnp.concatenate([key_grad[:, 1:], value_grad[:, 1:]], axis=3).reshape(
        requests, BLOCK, 2 * columns
    )
    returning = (
        jnp.zeros((shards * capacity, BLOCK, 2 * columns), jnp.float32).at[wanted].add(remote_grad)
    )
    returned = lax.all_to_all(returning, "ctx", split_axis=0, concat_axis=0, tiled=True)
    local_grad = jnp.concatenate([key_grad[:, 0], value_grad[:, 0]], axis=2)
    local_grad = local_grad.at[send_ids].add(jnp.where(filled[:, None, None], returned, 0.0))
    local_grad = local_grad.reshape(length, 2 * columns)
    grad_keys, grad_values = (
        lax.all_to_all(local_grad[:, :columns], "head", split_axis=0, concat_axis=1, tiled=True),
        lax.all_to_all(local_grad[:, columns:], "head", split_axis=0, concat_axis=1, tiled=True),
    )
    table_grad = (
        jnp.zeros(bias_table.shape, jnp.float32)
        .at[bias_index.reshape(-1)]
        .add(bias_grad.reshape(-1, BLOCK, BLOCK))
    )
    grad_table = lax.psum(table_grad, ("ctx", "head"))
    grad_gain = lax.psum(gain_grad, "ctx")
    return (attended, grad_queries, grad_keys, grad_values, grad_table, grad_gain)


def solution(mesh):
    return jax.shard_map(
        body,
        mesh=mesh,
        in_specs=(
            P(("ctx", "head"), None),
            P(("ctx", "head"), None),
            P(("ctx", "head"), None),
            P(("ctx", "head"), None),
            P(),
            P("ctx", None),
            P(),
            P("head"),
        ),
        out_specs=(
            P(("ctx", "head"), None),
            P(("ctx", "head"), None),
            P(("ctx", "head"), None),
            P(("ctx", "head"), None),
            P(),
            P("head"),
        ),
        check_vma=False,
    )
```

profile of v0, /device:TPU:1, one launch (start us, length us, event | category | flops | bytes accessed | tf_op | source)
XLA Modules:
  0.0 573.6 jit_solution(18262318619627758660)
XLA Ops:
  9.2 6.6 %all-to-all-start.1 = ((f32[128,8,96]{0,2,1:T(8,128)}), f32[128,8,96]{0,2,1:T(8,128)S(1)}, u32[]{:S(2)}, u32[]{:S(2)}) async-start(f32[128,8,96]{0,2,1:T(8,128)} %bitcast.3), calls=%async_computation.1 | async-start | bytes 786432 | tf_op jit(solution)/shard_map/all_to_all | solution.py:47
  19.0 4.5 all-to-all-done.1
  23.5 4.6 all-to-all-start
  28.1 7.7 %all-to-all-done = f32[128,8,96]{0,2,1:T(8,128)S(1)} async-done(((f32[128,8,96]{0,2,1:T(8,128)}), f32[128,8,96]{0,2,1:T(8,128)S(1)}, u32[]{:S(2)}, u32[]{:S(2)}) %all-to-all-start) | async-done | bytes 393248 | tf_op jit(solution)/shard_map/all_to_all | solution.py:46
  38.3 4.0 broadcast_select_fusion.1
  42.3 10.7 %all-to-all-start.2 = ((f32[32,128,192]{1,2,0:T(8,128)}), f32[32,128,192]{1,2,0:T(8,128)}, u32[]{:S(2)}, u32[]{:S(2)}) async-start(f32[32,128,192]{1,2,0:T(8,128)} %broadcast_select_fusion.1), calls=%async_computation.2 | async-start | bytes 6291456 | tf_op jit(solution)/shard_map/all_to_all | solution.py:65
  54.3 70.2 %all-to-all-done.2 = f32[32,128,192]{1,2,0:T(8,128)} async-done(((f32[32,128,192]{1,2,0:T(8,128)}), f32[32,128,192]{1,2,0:T(8,128)}, u32[]{:S(2)}, u32[]{:S(2)}) %all-to-all-start.2) | async-done | bytes 3145760 | tf_op jit(solution)/shard_map/all_to_all | solution.py:65
  124.5 7.4 %all-to-all-start.3 = ((f32[128,8,96]{0,2,1:T(8,128)}), f32[128,8,96]{0,2,1:T(8,128)S(1)}, u32[]{:S(2)}, u32[]{:S(2)}) async-start(f32[128,8,96]{0,2,1:T(8,128)} %bitcast.13), calls=%async_computation.3 | async-start | bytes 786432 | tf_op jit(solution)/shard_map/all_to_all | solution.py:45
  135.2 2.5 gather_fusion.1
  139.6 4.6 all-to-all-start.5
  144.2 7.1 %fusion.19 = (f32[8,2,128]{2,1,0:T(2,128)S(1)}, f32[8,2,128,3,128]{2,4,3,1,0:T(8,128)S(1)}) fusion(f32[8,128,3,128]{1,3,2,0:T(8,128)} %bitcast.132, f32[2]{0:T(128)S(1)} %copy-done.21, f32[8,128,2,48,1]{1,3,4,2,0:T(8,128)} %bitcast.145, f32[8,3,128,2,48]{2,4,3,1,0:T(8,128)} %bitcast.134), kind=kOutput, calls=%fused_computation.74 | convolution fusion | flops 456128512 | bytes 6299656 | tf_op jit(solution)/shard_map/jvp(vmap(ihd,mchd->himc))/dot_general | solution.py:21
  154.5 3.1 reshape.372
  158.3 6.8 %fusion = (f32[8,2,128]{2,1,0:T(2,128)S(1)}, f32[8,2,384,128]{3,2,1,0:T(8,128)S(1)}) fusion(f32[8,2,128,3,128]{2,4,3,1,0:T(8,128)S(1)} %get-tuple-element.50, f32[8,2,128]{2,1,0:T(2,128)} %multiply_divide_fusion, f32[8,2,128]{2,1,0:T(2,128)S(1)} %get-tuple-element.49, f32[8,384,2,48]{1,3,2,0:T(8,128)} %reshape.372, f32[8,2,48,128]{3,2,1,0:T(8,128)S(1)} %bitcast.143), kind=kOutput, calls=%fused_computation.8 | convolution fusion | flops 456128512 | bytes 7888896 | tf_op jit(solution)/shard_map/transpose(jvp(vmap(hik,khd->ihd)))/dot_general | solution.py:29
  165.1 2.9 multiply_reduce_fusion
  169.7 5.0 convolution_bitcast_fusion
  174.6 3.3 reshape.376
  177.9 5.1 convolution_bitcast_fusion.1
  185.9 4.0 scatter_fusion
  189.9 5.3 all-to-all-start.7
  196.5 5.2 fusion.20
  201.8 3.0 fusion.4
  204.8 61.3 %all-to-all-done.7 = f32[32,128,192]{1,2,0:T(8,128)} async-done(((f32[32,128,192]{1,2,0:T(8,128)}), f32[32,128,192]{1,2,0:T(8,128)}, u32[]{:S(2)}, u32[]{:S(2)}) %all-to-all-start.7) | async-done | bytes 3145760 | tf_op jit(solution)/shard_map/all_to_all | solution.py:98
  266.1 9.1 %all-to-all-start.4 = ((f32[8,128,96]{1,2,0:T(8,128)}), f32[8,128,96]{1,2,0:T(8,128)S(1)}, u32[]{:S(2)}, u32[]{:S(2)}) async-start(f32[8,128,96]{1,2,0:T(8,128)} %bitcast.23), calls=%async_computation.4 | async-start | bytes 786432 | tf_op jit(solution)/shard_map/all_to_all | solution.py:85
  275.2 4.0 broadcast_select_fusion
  279.2 5.6 scatter_fusion.1
  284.8 5.1 all-to-all-start.6
  291.6 6.0 %all-to-all-done.6 = f32[8,128,96]{1,2,0:T(8,128)S(1)} async-done(((f32[8,128,96]{1,2,0:T(8,128)}), f32[8,128,96]{1,2,0:T(8,128)S(1)}, u32[]{:S(2)}, u32[]{:S(2)}) %all-to-all-start.6) | async-done | bytes 393248 | tf_op jit(solution)/shard_map/all_to_all | solution.py:88
  297.6 4.6 all-to-all-start.8
  304.2 4.5 scatter_fusion.2
  311.6 4.8 all-to-all-start.9
  316.4 57.9 %psum.15 = f32[2]{0:T(128)} all-reduce(f32[2]{0:T(128)S(1)} %copy-done.27), channel_id=1, replica_groups=mesh['ctx'=32,'head'=8] {'ctx'}, use_global_device_ids=true, to_apply=%region_12.13 | all-reduce | flops 2 | bytes 16 | tf_op jit(solution)/shard_map/psum | solution.py:112
  378.0 186.3 %all-reduce.2.cloned.1.call-done = f32[16,128,128]{2,1,0:T(8,128)} async-done(((f32[16,128,128]{2,1,0:T(8,128)}), f32[16,128,128]{2,1,0:T(8,128)}) %all-reduce.2.cloned.1.call-update) | async-done | bytes 1048592 | tf_op jit(solution)/shard_map/psum | solution.py:111
  (123 shorter events, 36.3 us)
Async XLA Ops:
  7.2 124.7 %copy-start = (f32[16,128,128]{2,1,0:T(8,128)S(1)}, f32[16,128,128]{2,1,0:T(8,128)}, u32[]{:S(2)}) copy-start(f32[16,128,128]{2,1,0:T(8,128)} %param.14) | copy-start | bytes 3145732
  9.2 14.3 %all-to-all-start.1 = ((f32[128,8,96]{0,2,1:T(8,128)}), f32[128,8,96]{0,2,1:T(8,128)S(1)}, u32[]{:S(2)}, u32[]{:S(2)}) async-start(f32[128,8,96]{0,2,1:T(8,128)} %bitcast.3), calls=%async_computation.1 | async-start | bytes 786432 | tf_op jit(solution)/shard_map/all_to_all | solution.py:47
  19.0 19.3 %copy-start.19 = (pred[32]{0:T(512)(128)(4,1)}, pred[32]{0:T(512)(128)(4,1)S(1)}, u32[]{:S(2)}) copy-start(pred[32]{0:T(512)(128)(4,1)S(1)} %get-tuple-element.39) | copy-start | bytes 100
  23.5 12.3 %all-to-all-start = ((f32[128,8,96]{0,2,1:T(8,128)}), f32[128,8,96]{0,2,1:T(8,128)S(1)}, u32[]{:S(2)}, u32[]{:S(2)}) async-start(f32[128,8,96]{0,2,1:T(8,128)} %bitcast), calls=%async_computation | async-start | bytes 786432 | tf_op jit(solution)/shard_map/all_to_all | solution.py:46
  28.1 10.2 %copy-start.23 = (s32[32]{0:T(128)}, s32[32]{0:T(128)S(1)}, u32[]{:S(2)}) copy-start(s32[32]{0:T(128)S(1)} %fusion.14) | copy-start | bytes 388
  42.3 10.7 %copy-start.17 = (s32[8,3]{0,1:T(4,128)S(1)}, s32[8,3]{0,1:T(4,128)}, u32[]{:S(2)}) copy-start(s32[8,3]{0,1:T(4,128)} %param.13) | copy-start | bytes 292
  42.3 10.9 %copy-start.15 = (f32[128,768]{1,0:T(8,128)S(1)}, f32[128,768]{1,0:T(8,128)}, u32[]{:S(2)}) copy-start(f32[128,768]{1,0:T(8,128)} %param.8) | copy-start | bytes 1179652
  42.3 82.2 %all-to-all-start.2 = ((f32[32,128,192]{1,2,0:T(8,128)}), f32[32,128,192]{1,2,0:T(8,128)}, u32[]{:S(2)}, u32[]{:S(2)}) async-start(f32[32,128,192]{1,2,0:T(8,128)} %broadcast_select_fusion.1), calls=%async_computation.2 | async-start | bytes 6291456 | tf_op jit(solution)/shard_map/all_to_all | solution.py:65
  54.2 70.3 %copy-start.25 = (s32[16]{0:T(128)}, s32[16]{0:T(128)S(1)}, u32[]{:S(2)}) copy-start(s32[16]{0:T(128)S(1)} %fusion.15) | copy-start | bytes 196
  124.5 15.1 %all-to-all-start.3 = ((f32[128,8,96]{0,2,1:T(8,128)}), f32[128,8,96]{0,2,1:T(8,128)S(1)}, u32[]{:S(2)}, u32[]{:S(2)}) async-start(f32[128,8,96]{0,2,1:T(8,128)} %bitcast.13), calls=%async_computation.3 | async-start | bytes 786432 | tf_op jit(solution)/shard_map/all_to_all | solution.py:45
  137.7 6.4 %copy-start.21 = (f32[2]{0:T(128)S(1)}, f32[2]{0:T(128)}, u32[]{:S(2)}) copy-start(f32[2]{0:T(128)} %param.15) | copy-start | bytes 28
  139.6 4.6 copy-start.12
  139.6 18.7 %all-to-all-start.5 = ((f32[128,8,96]{0,2,1:T(8,128)}), f32[128,8,96]{0,2,1:T(8,128)S(1)}, u32[]{:S(2)}, u32[]{:S(2)}) async-start(f32[128,8,96]{0,2,1:T(8,128)} %bitcast.154), calls=%async_computation.5 | async-start | bytes 786432 | tf_op jit(solution)/shard_map/all_to_all | solution.py:48
  158.3 6.8 %copy-start.5 = (f32[8,3,128,128]{2,3,1,0:T(8,128)S(1)}, f32[8,3,128,128]{2,3,1,0:T(8,128)}, u32[]{:S(2)}) copy-start(f32[8,3,128,128]{2,3,1,0:T(8,128)} %copy.170) | copy-start | bytes 4718596
  158.3 6.9 %copy-start.22 = (f32[2]{0:T(128)S(1)}, f32[2]{0:T(128)}, u32[]{:S(2)}) copy-start(f32[2]{0:T(128)} %param.15) | copy-start | bytes 28
  168.4 9.5 %copy-start.2 = (f32[8,2,128,384]{2,3,1,0:T(8,128)}, f32[8,2,128,384]{2,3,1,0:T(8,128)S(1)}, u32[]{:S(2)}) copy-start(f32[8,2,128,384]{2,3,1,0:T(8,128)S(1)} %broadcast_multiply_fusion) | copy-start | bytes 9437188
  177.9 5.2 copy-start.10
  189.9 5.3 copy-start.18
  189.9 5.5 slice-start
  189.9 76.2 %all-to-all-start.7 = ((f32[32,128,192]{1,2,0:T(8,128)}), f32[32,128,192]{1,2,0:T(8,128)}, u32[]{:S(2)}, u32[]{:S(2)}) async-start(f32[32,128,192]{1,2,0:T(8,128)} %scatter_fusion), calls=%async_computation.7 | async-start | bytes 6291456 | tf_op jit(solution)/shard_map/all_to_all | solution.py:98
  195.5 6.3 %copy-start.3 = (f32[8,2,128,384]{2,3,1,0:T(8,128)S(1)}, f32[8,2,128,384]{2,3,1,0:T(8,128)}, u32[]{:S(2)}) copy-start(f32[8,2,128,384]{2,3,1,0:T(8,128)} %copy-done.2) | copy-start | bytes 9437188
  195.5 6.3 %copy-start.7 = (f32[8,3,128,96]{2,3,1,0:T(8,128)S(1)}, f32[8,3,128,96]{2,3,1,0:T(8,128)}, u32[]{:S(2)}) copy-start(f32[8,3,128,96]{2,3,1,0:T(8,128)} %get-tuple-element.42) | copy-start | bytes 3538948
  201.8 73.4 %copy-start.20 = (pred[32]{0:T(512)(128)(4,1)S(1)}, pred[32]{0:T(512)(128)(4,1)}, u32[]{:S(2)}) copy-start(pred[32]{0:T(512)(128)(4,1)} %copy-done.19) | copy-start | bytes 100
  266.1 18.6 %all-to-all-start.4 = ((f32[8,128,96]{1,2,0:T(8,128)}), f32[8,128,96]{1,2,0:T(8,128)S(1)}, u32[]{:S(2)}, u32[]{:S(2)}) async-start(f32[8,128,96]{1,2,0:T(8,128)} %bitcast.23), calls=%async_computation.4 | async-start | bytes 786432 | tf_op jit(solution)/shard_map/all_to_all | solution.py:85
  275.2 4.0 copy-start.24
  284.7 17.4 %copy-start.9 = (f32[8,128,384]{1,2,0:T(8,128)S(1)}, f32[8,128,384]{1,2,0:T(8,128)}, u32[]{:S(2)}) copy-start(f32[8,128,384]{1,2,0:T(8,128)} %get-tuple-element.37) | copy-start | bytes 4718596
  284.8 12.8 %all-to-all-start.6 = ((f32[8,128,96]{1,2,0:T(8,128)}), f32[8,128,96]{1,2,0:T(8,128)S(1)}, u32[]{:S(2)}, u32[]{:S(2)}) async-start(f32[8,128,96]{1,2,0:T(8,128)} %bitcast.36), calls=%async_computation.6 | async-start | bytes 786432 | tf_op jit(solution)/shard_map/all_to_all | solution.py:88
  297.6 14.0 %all-to-all-start.8 = ((f32[8,128,96]{1,2,0:T(8,128)}), f32[8,128,96]{1,2,0:T(8,128)S(1)}, u32[]{:S(2)}, u32[]{:S(2)}) async-start(f32[8,128,96]{1,2,0:T(8,128)} %bitcast.129), calls=%async_computation.8 | async-start | bytes 786432 | tf_op jit(solution)/shard_map/all_to_all | solution.py:103
  302.2 262.2 %all-reduce.2.cloned.1.call-start = ((), (), s32[]{:S(2)}) async-start(), calls=%async_computation.10 | async-start | bytes 2097152 | tf_op jit(solution)/shard_map/psum | solution.py:111
  304.2 12.2 %copy-start.27 = (f32[2]{0:T(128)S(1)}, f32[2]{0:T(128)}, u32[]{:S(2)}) copy-start(f32[2]{0:T(128)} %get-tuple-element.36) | copy-start | bytes 28
  309.7 256.9 %copy-start.1 = (f32[16,128,128]{2,1,0:T(8,128)S(1)}, f32[16,128,128]{2,1,0:T(8,128)}, u32[]{:S(2)}) copy-start(f32[16,128,128]{2,1,0:T(8,128)} %param.14) | copy-start | bytes 3145732
  311.6 65.5 %all-to-all-start.9 = ((f32[8,128,96]{1,2,0:T(8,128)}), f32[8,128,96]{1,2,0:T(8,128)S(1)}, u32[]{:S(2)}, u32[]{:S(2)}) async-start(f32[8,128,96]{1,2,0:T(8,128)} %bitcast.128), calls=%async_computation.9 | async-start | bytes 786432 | tf_op jit(solution)/shard_map/all_to_all | solution.py:104
  (8 other events, 14.1 us)
Sparse Core Ops, SparseCore 0:
  309.8 254.4 all-reduce.1
where the time goes:
time: 583 us; the launch traced here: 574 us
  waiting for transfers between devices  336 us (58%)
  starting transfers between devices  62.6 us (11%)
  blocking collectives  57.9 us (10%)
  local copies, waits for them, and re-layouts  41.1 us (7%)
  matrix products  32.2 us (6%)
  other arithmetic  28.8 us (5%)
  between operations  14.7 us (3%)
    psum x1, waiting for transfers between devices, body(): grad_table = lax.psum(table_grad, ('ctx', 'head'))  186 us
    all_to_all x1, waiting for transfers between devices, body(): lax.all_to_all(outgoing, 'ctx', split_axis=0, concat_axis=0, tiled=True)  70.2 us
    all_to_all x1, waiting for transfers between devices, body(): lax.all_to_all(returning, 'ctx', split_axis=0, concat_axis=0, tiled=True)  61.3 us
    psum x1, blocking collectives, body(): grad_gain = lax.psum(gain_grad, 'ctx')  57.9 us
    unnamed x69, local copies, waits for them, and re-layouts  17.6 us
    dot_general x3, matrix products, attend(): jnp.einsum('hik,khd->ihd', weights, value_heads, precision=lax.Precision....  17 us
    dot_general x3, matrix products, attend(): jnp.einsum('ihd,mchd->himc', query_heads, key_heads, precision=lax.Precis...  15.2 us
  transfers between devices with their start and end apart: 11, of which 7 were waited for; matrix products, arithmetic and copies ran while one was open for 10% of the time, Pallas kernels for 0%

commit v1 on v0

v1 whole, which is shorter than its diff:
```python
import jax
import jax.numpy as jnp
from jax import lax
from jax.experimental import pallas as pl
from jax.experimental.pallas import tpu as pltpu
from jax.sharding import PartitionSpec as P

BLOCK = 128
NEI = 2
HEADS = 2
MESH = pl.DeviceIdType.MESH
HIGHEST = lax.Precision.HIGHEST


def mm(a, b, ca, cb):
    return lax.dot_general(
        a, b, (((ca,), (cb,)), ((), ())), precision=HIGHEST, preferred_element_type=jnp.float32
    )


def make_kernel(nx, nz, nh, nbias, dim):
    nc = nx * nz
    blocks = nh
    requests = blocks * NEI
    pair = 2 * dim
    width = HEADS * dim
    share = nbias // nh
    piece = share * BLOCK // nc
    factor = dim ** (-0.5)

    def kernel(
        sid, rof, weight, nbr, bidx, gain,
        q_in, k_in, v_in, g_in, table,
        o_out, dq_out, dk_out, dv_out, table_out, gain_out,
        tkv, tqd, kv, qd,
        out0, out1, arr0, arr1, ret0, ret1, back0, back1, g0, g1,
        loc, oq, oqin, dkvin, ds, gacc, tl, trs, tsum, tb, tbin, tc,
        s_kv, r_kv, s_qd, r_qd, s_x0, r_x0, s_x1, r_x1, s_b0, r_b0, s_b1, r_b1,
        s_oq, r_oq, s_dkv, r_dkv, s_ta, r_ta, s_tb, r_tb, s_tc, r_tc, s_td, r_td,
    ):
        c = lax.axis_index("ctx")
        k = lax.axis_index("head")
        x = c // nz
        z = c % nz

        def there(o):
            return ((x + o // nz) % nx) * nz + (z + o % nz) % nz

        def source(o):
            return ((x + nx - o // nz) % nx) * nz + (z + nz - o % nz) % nz

        def peer(i):
            return (k + i) % nh

        barrier = pltpu.get_barrier_semaphore()

        @pl.loop(1, nh)
        def _(i):
            pl.semaphore_signal(barrier, inc=1, device_id=(c, peer(i)), device_id_type=MESH)

        @pl.loop(1, nc)
        def _(o):
            pl.semaphore_signal(barrier, inc=1, device_id=(there(o), k), device_id_type=MESH)

        def turn(first, second, dst):
            for j in range(nh):
                if width % 8 == 0 and (j * width) // 128 == (j * width + width - 1) // 128:
                    pass
            for n, ref in enumerate((first, second)):
                full = jnp.transpose(ref[...])
                for j in range(nh):
                    for h in range(HEADS):
                        row = j * width + h * dim
                        dst[j, h, n * dim : (n + 1) * dim, :] = full[row : row + dim, :]

        def to_head(src, dst, ssem, rsem, i):
            return pltpu.make_async_remote_copy(
                src.at[peer(i)], dst.at[k], ssem.at[i], rsem.at[i],
                device_id=(c, peer(i)), device_id_type=MESH,
            )

        turn(k_in, v_in, tkv)
        pl.semaphore_wait(barrier, nh + nc - 2)

        @pl.loop(1, nh)
        def _(i):
            to_head(tkv, kv, s_kv, r_kv, i).start()

        turn(q_in, g_in, tqd)

        @pl.loop(1, nh)
        def _(i):
            to_head(tqd, qd, s_qd, r_qd, i).start()

        kv[k] = tkv[k]
        qd[k] = tqd[k]

        @pl.loop(1, nh)
        def _(i):
            to_head(tkv, kv, s_kv, r_kv, i).wait_recv()

        def exchange(src, dst, ssem, rsem, o):
            return pltpu.make_async_remote_copy(
                src.at[o], dst.at[o], ssem.at[o], rsem.at[o],
                device_id=(there(o), k), device_id_type=MESH,
            )

        def give_back(src, dst, ssem, rsem, o):
            return pltpu.make_async_remote_copy(
                src.at[o], dst.at[o], ssem.at[o], rsem.at[o],
                device_id=(source(o), k), device_id_type=MESH,
            )

        for h, out, arr, ssem, rsem in ((0, out0, arr0, s_x0, r_x0), (1, out1, arr1, s_x1, r_x1)):

            @pl.loop(1, nc)
            def _(o):
                out[o] = kv[sid[there(o)], h]
                exchange(out, arr, ssem, rsem, o).start()

        @pl.loop(1, nh)
        def _(i):
            to_head(tqd, qd, s_qd, r_qd, i).wait_recv()

        gacc[...] = jnp.zeros_like(gacc)

        def attend(b, h, arr, g):
            gain_h = gain[h]
            qt = qd[b, h, 0:dim, :] * factor
            dot = qd[b, h, dim:pair, :]
            q = jnp.transpose(qt)
            do = jnp.transpose(dot)
            sets = [kv[b, h]]
            for m in range(NEI):
                owner = nbr[b * NEI + m] // blocks
                ox = (x + nx - owner // nz) % nx
                oz = (z + nz - owner % nz) % nz
                sets.append(arr[ox * nz + oz])
            bias = [table[bidx[b * (NEI + 1) + m]] for m in range(NEI + 1)]
            scores = [mm(q, t[0:dim], 1, 0) + gain_h * e for t, e in zip(sets, bias)]
            top = jnp.max(scores[0], axis=1, keepdims=True)
            for s in scores[1:]:
                top = jnp.maximum(top, jnp.max(s, axis=1, keepdims=True))
            weights = [jnp.exp(s - top) for s in scores]
            total = sum(jnp.sum(w, axis=1, keepdims=True) for w in weights)
            inverse = 1.0 / total
            weights = [w * inverse for w in weights]
            wgrad = [mm(do, t[dim:pair], 1, 0) for t in sets]
            delta = sum(jnp.sum(w * d, axis=1, keepdims=True) for w, d in zip(weights, wgrad))
            sgrad = [w * (d - delta) for w, d in zip(weights, wgrad)]
            oq[b, h, 0:dim, :] = sum(mm(t[dim:pair], w, 1, 1) for t, w in zip(sets, weights))
            oq[b, h, dim:pair, :] = factor * sum(mm(t[0:dim], s, 1, 1) for t, s in zip(sets, sgrad))
            part = jnp.zeros((8, BLOCK), jnp.float32)
            for m in range(NEI + 1):
                dk = mm(qt, sgrad[m], 1, 0)
                dv = mm(dot, weights[m], 1, 0)
                if m == 0:
                    loc[b, h, 0:dim, :] = dk
                    loc[b, h, dim:pair, :] = dv
                else:
                    g[b * NEI + m - 1, 0:dim, :] = dk
                    g[b * NEI + m - 1, dim:pair, :] = dv
                scaled = gain_h * sgrad[m]
                if h == 0:
                    ds[b * (NEI + 1) + m] = scaled
                else:
                    ds[b * (NEI + 1) + m] += scaled
                prod = sgrad[m] * bias[m]
                part = part + jnp.sum(prod.reshape(BLOCK // 8, 8, BLOCK), axis=0)
            gacc[h] += part

        def send_oq(h, i):
            return pltpu.make_async_remote_copy(
                oq.at[peer(i), h], oqin.at[k, h], s_oq.at[h, i], r_oq.at[h, i],
                device_id=(c, peer(i)), device_id_type=MESH,
            )

        def send_dkv(h, i):
            return pltpu.make_async_remote_copy(
                loc.at[peer(i), h], dkvin.at[k, h], s_dkv.at[h, i], r_dkv.at[h, i],
                device_id=(c, peer(i)), device_id_type=MESH,
            )

        for h, out, arr, ssem, rsem, g, ret, back, sb, rb in (
            (0, out0, arr0, s_x0, r_x0, g0, ret0, back0, s_b0, r_b0),
            (1, out1, arr1, s_x1, r_x1, g1, ret1, back1, s_b1, r_b1),
        ):

            @pl.loop(1, nc)
            def _(o):
                exchange(out, arr, ssem, rsem, o).wait_recv()

            @pl.loop(0, blocks)
            def _(b):
                attend(b, h, arr, g)

            @pl.loop(1, nc)
            def _(o):
                ret[o] = g[rof[source(o)]]
                give_back(ret, back, sb, rb, o).start()

            @pl.loop(1, nh)
            def _(i):
                send_oq(h, i).start()

            oqin[k, h] = oq[k, h]

        @pl.loop(0, nbias)
        def _(t):
            acc = jnp.zeros((BLOCK, BLOCK), jnp.float32)
            for r in range(blocks * (NEI + 1)):
                acc = acc + ds[r] * (bidx[r] == t).astype(jnp.float32)
            tl[t] = acc

        def table_head(i):
            return pltpu.make_async_remote_copy(
                tl.at[pl.ds(peer(i) * share, share)], trs.at[k], s_ta.at[i], r_ta.at[i],
                device_id=(c, peer(i)), device_id_type=MESH,
            )

        def table_ctx(o):
            return pltpu.make_async_remote_copy(
                tb.at[there(o)], tbin.at[c], s_tb.at[o], r_tb.at[o],
                device_id=(there(o), k), device_id_type=MESH,
            )

        def table_gather(o):
            return pltpu.make_async_remote_copy(
                tc.at[c], tc.at[c], s_tc.at[o], r_tc.at[o],
                device_id=(there(o), k), device_id_type=MESH,
            )

        def table_spread(i):
            return pltpu.make_async_remote_copy(
                tsum, table_out.at[pl.ds(k * share, share)], s_td.at[i], r_td.at[i],
                device_id=(c, peer(i)), device_id_type=MESH,
            )

        @pl.loop(1, nh)
        def _(i):
            table_head(i).start()

        trs[k] = tl[pl.ds(k * share, share)]

        @pl.loop(1, nh)
        def _(i):
            table_head(i).wait_recv()

        mine = jnp.concatenate(
            [jnp.sum(gacc[h], axis=0, keepdims=True) for h in range(HEADS)]
            + [jnp.zeros((8 - HEADS, BLOCK), jnp.float32)],
            axis=0,
        )

        @pl.loop(0, share)
        def _(t):
            acc = trs[0, t]
            for i in range(1, nh):
                acc = acc + trs[i, t]
            tsum[t] = acc

        per = BLOCK // piece

        @pl.loop(0, nc)
        def _(d):
            tb[d, 0:piece, :] = tsum[d // per, pl.ds(pl.multiple_of((d % per) * piece, 8), piece), :]
            tb[d, piece : piece + 8, :] = mine

        @pl.loop(1, nc)
        def _(o):
            table_ctx(o).start()

        tbin[c] = tb[c]

        def collect(h, back):
            @pl.loop(0, blocks)
            def _(b):
                acc = loc[b, h]
                for o in range(1, nc):
                    acc = acc + back[o] * weight[there(o) * blocks + b]
                loc[b, h] = acc

            @pl.loop(1, nh)
            def _(i):
                send_dkv(h, i).start()

            dkvin[k, h] = loc[k, h]

        @pl.loop(1, nc)
        def _(o):
            give_back(ret0, back0, s_b0, r_b0, o).wait_recv()

        collect(0, back0)

        @pl.loop(1, nc)
        def _(o):
            table_ctx(o).wait_recv()

        acc = tbin[0]
        for i in range(1, nc):
            acc = acc + tbin[i]
        tc[c] = acc[0:piece]
        gain_out[...] = jnp.broadcast_to(
            jnp.sum(acc[piece : piece + 8], axis=1, keepdims=True), (8, BLOCK)
        )

        @pl.loop(1, nc)
        def _(o):
            table_gather(o).start()

        @pl.loop(1, nc)
        def _(o):
            give_back(ret1, back1, s_b1, r_b1, o).wait_recv()

        collect(1, back1)

        @pl.loop(1, nc)
        def _(o):
            table_gather(o).wait_recv()

        @pl.loop(0, nc)
        def _(d):
            tsum[d // per, pl.ds(pl.multiple_of((d % per) * piece, 8), piece), :] = tc[d]

        @pl.loop(1, nh)
        def _(i):
            table_spread(i).start()

        table_out[pl.ds(k * share, share)] = tsum[...]

        def restore(src, first, second):
            for n, ref in enumerate((first, second)):
                rows = []
                for j in range(nh):
                    for h in range(HEADS):
                        rows.append(src[j, h, n * dim : (n + 1) * dim, :])
                ref[...] = jnp.transpose(jnp.concatenate(rows, axis=0))

        for h in range(HEADS):

            @pl.loop(1, nh)
            def _(i):
                send_oq(h, i).wait_recv()

        restore(oqin, o_out, dq_out)

        for h in range(HEADS):

            @pl.loop(1, nh)
            def _(i):
                send_dkv(h, i).wait_recv()

        restore(dkvin, dk_out, dv_out)

        @pl.loop(1, nh)
        def _(i):
            to_head(tkv, kv, s_kv, r_kv, i).wait_send()
            to_head(tqd, qd, s_qd, r_qd, i).wait_send()
            table_head(i).wait_send()
            table_spread(i).wait()
            for h in range(HEADS):
                send_oq(h, i).wait_send()
                send_dkv(h, i).wait_send()

        @pl.loop(1, nc)
        def _(o):
            exchange(out0, arr0, s_x0, r_x0, o).wait_send()
            exchange(out1, arr1, s_x1, r_x1, o).wait_send()
            give_back(ret0, back0, s_b0, r_b0, o).wait_send()
            give_back(ret1, back1, s_b1, r_b1, o).wait_send()
            table_ctx(o).wait_send()
            table_gather(o).wait_send()

    def f32(*shape):
        return pltpu.VMEM(shape, jnp.float32)

    def sems(*shape):
        return pltpu.SemaphoreType.DMA(shape)

    scratch = (
        [f32(nh, HEADS, pair, BLOCK)] * 4
        + [f32(nc, pair, BLOCK)] * 8
        + [f32(requests, pair, BLOCK)] * 2
        + [f32(nh, HEADS, pair, BLOCK)] * 4
        + [f32(blocks * (NEI + 1), BLOCK, BLOCK), f32(HEADS, 8, BLOCK)]
        + [f32(nbias, BLOCK, BLOCK), f32(nh, share, BLOCK, BLOCK), f32(share, BLOCK, BLOCK)]
        + [f32(nc, piece + 8, BLOCK)] * 2
        + [f32(nc, piece, BLOCK)]
        + [sems(nh)] * 4
        + [sems(nc)] * 8
        + [sems(HEADS, nh)] * 4
        + [sems(nh)] * 2
        + [sems(nc)] * 4
        + [sems(nh)] * 2
    )
    return kernel, scratch


def solution(mesh):
    nc = mesh.shape["ctx"]
    nh = mesh.shape["head"]
    nx = 4
    nz = nc // nx

    def body(queries, keys, values, grad_out, neighbours, bias_index, bias_table, head_gain):
        rows, columns = queries.shape
        nbias = bias_table.shape[0]
        dim = columns // (nh * HEADS)
        blocks = nh
        requests = blocks * NEI
        me = lax.axis_index("ctx")
        asks = neighbours.reshape(nc, requests)
        owner = asks // blocks
        local = asks % blocks
        hit = (owner == me)[:, :, None] & (local[:, :, None] == jnp.arange(blocks)[None, None, :])
        weight = jnp.max(hit.astype(jnp.float32), axis=1)
        sid = jnp.max(jnp.where(owner == me, local, 0), axis=1)
        own = lax.dynamic_index_in_dim(asks, me, 0, keepdims=False)
        wanted = (own // blocks)[None, :] == jnp.arange(nc)[:, None]
        rof = jnp.max(jnp.where(wanted, jnp.arange(requests)[None, :], 0), axis=1)
        kernel, scratch = make_kernel(nx, nz, nh, nbias, dim)
        smem = pl.BlockSpec(memory_space=pltpu.SMEM)
        vmem = pl.BlockSpec(memory_space=pltpu.VMEM)
        wide = jax.ShapeDtypeStruct((rows, columns), jnp.float32)
        outs = pl.pallas_call(
            kernel,
            out_shape=[wide] * 4
            + [
                jax.ShapeDtypeStruct(bias_table.shape, jnp.float32),
                jax.ShapeDtypeStruct((8, BLOCK), jnp.float32),
            ],
            in_specs=[smem] * 6 + [vmem] * 5,
            out_specs=[vmem] * 6,
            scratch_shapes=scratch,
            compiler_params=pltpu.CompilerParams(
                collective_id=0, has_side_effects=True, vmem_limit_bytes=60 * 1024 * 1024
            ),
        )(
            sid, rof, weight.reshape(-1), own, bias_index.reshape(-1), head_gain,
            queries, keys, values, grad_out, bias_table,
        )
        return (*outs[:5], outs[5][:HEADS, 0])

    return jax.shard_map(
        body,
        mesh=mesh,
        in_specs=(
            P(("ctx", "head"), None),
            P(("ctx", "head"), None),
            P(("ctx", "head"), None),
            P(("ctx", "head"), None),
            P(),
            P("ctx", None),
            P(),
            P("head"),
        ),
        out_specs=(
            P(("ctx", "head"), None),
            P(("ctx", "head"), None),
            P(("ctx", "head"), None),
            P(("ctx", "head"), None),
            P(),
            P("head"),
        ),
        check_vma=False,
    )
```

time: 583 us -> 208 us (0.36); the launches traced: 574 us -> 207 us
  waiting for transfers between devices: 336 us -> 0 us
  Pallas kernels: 0 us -> 195 us
  starting transfers between devices: 62.6 us -> 0 us
  blocking collectives: 57.9 us -> 0 us
  matrix products: 32.2 us -> 0 us
  local copies, waits for them, and re-layouts: 41.1 us -> 9.86 us
  other arithmetic: 28.8 us -> 1.84 us
  between operations: 14.7 us -> 0.69 us
    pallas_call x0 -> x1, Pallas kernels: none -> 195 us  [body(): pl.pallas_call(kernel, out_shape=[wide] * 4 + [jax.ShapeDtypeStruct(bias_...]
    psum x1 -> x0, waiting for transfers between devices: 186 us -> none  [body(): grad_table = lax.psum(table_grad, ('ctx', 'head'))]
    all_to_all x10 -> x0, waiting for transfers between devices: 150 us -> none  [the longest x1 70.2 us: body(): lax.all_to_all(outgoing, 'ctx', split_axis=0, concat_axis=0, tiled=True)]
    all_to_all x10 -> x0, starting transfers between devices: 62.6 us -> none  [the longest x1 10.7 us: body(): lax.all_to_all(outgoing, 'ctx', split_axis=0, concat_axis=0, tiled=True)]
    psum x1 -> x0, blocking collectives: 57.9 us -> none  [body(): grad_gain = lax.psum(gain_grad, 'ctx')]
    dot_general x6 -> x0, matrix products: 32.2 us -> none  [the longest x3 17 us: attend(): jnp.einsum('hik,khd->ihd', weights, value_heads, precision=lax.Precision....]
    scatter-add x3 -> x0, other arithmetic: 14.1 us -> none  [the longest x1 5.56 us: body(): local_grad.at[send_ids].add(jnp.where(filled[:, None, None], returned, 0.0))]
    unnamed x69 -> x19, local copies, waits for them, and re-layouts: 17.6 us -> 6.99 us
  transfers between devices with their start and end apart: 11 -> 0, of which waited for: 7 -> 0; matrix products, arithmetic and copies ran while one was open for 10% -> 0% of each run, Pallas kernels for 0% -> 0%
where the time goes in v1:
time: 208 us; the launch traced here: 207 us
  Pallas kernels  195 us (94%)
  local copies, waits for them, and re-layouts  9.86 us (5%)
    pallas_call x1, Pallas kernels, body(): pl.pallas_call(kernel, out_shape=[wide] * 4 + [jax.ShapeDtypeStruct(bias_...  195 us
    unnamed x19, local copies, waits for them, and re-layouts  6.99 us

profile of v1, /device:TPU:1, one launch (start us, length us, event | category | flops | bytes accessed | tf_op | source)
XLA Modules:
  0.0 207.3 jit_solution(13564297579038298071)
XLA Ops:
  0.6 0.0 copy-start.4
  0.6 0.7 copy-done.4
  1.3 0.0 copy-start.5
  1.3 0.7 copy-done.5
  2.0 0.1 copy.28
  2.1 0.6 reshape.74.bidx
  2.7 0.1 reduce_max.35
  2.8 0.6 reduce_max.36.sid
  3.4 0.1 copy.22
  3.5 0.1 reshape.72
  3.6 0.5 fusion.6
  4.2 0.1 copy.23
  4.2 0.6 select_reduce_fusion.rof
  4.9 0.1 copy.27
  5.0 0.7 reshape.73.weight
  5.6 194.9 %shard_map.127 = (f32[128,768]{1,0:T(8,128)}, f32[128,768]{1,0:T(8,128)}, f32[128,768]{1,0:T(8,128)}, f32[128,768]{1,0:T(8,128)}, f32[16,128,128]{2,1,0:T(8,128)}, /*index=5*/f32[8,128]{1,0:T(8,128)}) custom-call(s32[32]{0:T(128)} %reduce_max.36.sid, s32[32]{0:T(128)} %select_reduce_fusion.rof, f32[256]{0:T(256)} %reshape.73.weight, ...), custom_call_target="tpu_custom_call" | custom-call | tf_op jit(solution)/shard_map/pallas_call | solution.py:425
  200.6 1.3 slice_reduce_fusion
  201.9 0.0 copy-start.3
  201.9 0.0 copy-start.2
  201.9 1.8 copy.34
  203.7 0.0 copy-done.3
  203.7 0.0 copy-start
  203.7 0.7 copy.35
  204.4 0.0 copy-done.2
  204.5 0.0 copy-start.1
  204.5 0.7 copy.36
  205.2 0.4 copy-done.1
  205.6 0.7 copy.37
  206.3 0.0 copy-done
  206.3 1.0 copy.38
  (4 shorter events, 0.1 us)
Async XLA Ops:
  0.6 0.7 copy-start.4
  1.3 0.7 copy-start.5
  201.9 1.8 copy-start.3
  201.9 2.6 %copy-start.2 = (f32[128,768]{1,0:T(8,128)S(1)}, f32[128,768]{1,0:T(8,128)}, u32[]{:S(2)}) copy-start(f32[128,768]{1,0:T(8,128)} %get-tuple-element.28) | copy-start | bytes 1179652
  203.7 2.6 %copy-start = (f32[16,128,128]{2,1,0:T(8,128)S(1)}, f32[16,128,128]{2,1,0:T(8,128)}, u32[]{:S(2)}) copy-start(f32[16,128,128]{2,1,0:T(8,128)} %get-tuple-element.30) | copy-start | bytes 3145732
  204.5 1.1 copy-start.1

commit v2 on v1

v2 whole, which is shorter than its diff:
```python
import jax
import jax.numpy as jnp
from jax import lax
from jax.experimental import pallas as pl
from jax.experimental.pallas import tpu as pltpu
from jax.sharding import PartitionSpec as P

BLOCK = 128
NEI = 2
HEADS = 2
MESH = pl.DeviceIdType.MESH
HIGHEST = lax.Precision.HIGHEST


def mm(a, b, ca, cb):
    return lax.dot_general(
        a, b, (((ca,), (cb,)), ((), ())), precision=HIGHEST, preferred_element_type=jnp.float32
    )


def make_kernel(nx, nz, nh, nbias, dim):
    nc = nx * nz
    blocks = nh
    requests = blocks * NEI
    pair = 2 * dim
    width = HEADS * dim
    share = nbias // nh
    piece = share * BLOCK // nc
    factor = dim ** (-0.5)

    def kernel(
        key, rof, nbr, bidx, gain,
        q_in, k_in, v_in, g_in, table,
        o_out, dq_out, dk_out, dv_out, table_out, gain_out,
        tkv, tqd, kv0, kv1, qd, loc, oq, oqin, dkvin,
        ds, gacc, tl, trs, tsum, tb, tbin, tc,
        s_kv, r_kv, s_qd, r_qd, s_oq, r_oq, s_dkv, r_dkv,
        s_ta, r_ta, s_tb, r_tb, s_tc, r_tc, s_td, r_td,
        s_f, r_f, r_h, s_x, r_x, s_g, r_g, r_b, s_y, r_y,
        *rest,
    ):
        kv = (kv0, kv1)
        hops = [[rest[(h * 2 + s) * 5 : (h * 2 + s) * 5 + 5] for s in range(2)] for h in range(HEADS)]
        rest = rest[HEADS * 10 :]
        backs = [[rest[(h * 2 + s) * 6 : (h * 2 + s) * 6 + 6] for s in range(2)] for h in range(HEADS)]
        rest = rest[HEADS * 12 :]
        flat = [rest[h * 5 : h * 5 + 5] for h in range(HEADS)]

        c = lax.axis_index("ctx")
        k = lax.axis_index("head")
        x = c // nz
        z = c % nz

        def at(dx, dz):
            return ((x + nx + dx) % nx) * nz + (z + nz + dz) % nz

        def peer(i):
            return (k + i) % nh

        def wants(src, dst):
            return key[src * nc + dst]

        def pick(src, dst):
            return jnp.maximum(wants(src, dst), 0)

        def is_block(src, dst, b):
            return (wants(src, dst) == b).astype(jnp.float32)

        def remote(src, dst, ssem, rsem, dev):
            return pltpu.make_async_remote_copy(
                src, dst, ssem, rsem, device_id=dev, device_id_type=MESH
            )

        barrier = pltpu.get_barrier_semaphore()

        @pl.loop(1, nh)
        def _(i):
            pl.semaphore_signal(barrier, inc=1, device_id=(c, peer(i)), device_id_type=MESH)

        near = [at(ox, 0) for ox in range(1, nx)] + [at(0, 1), at(0, -1)]
        for d in near:
            pl.semaphore_signal(barrier, inc=1, device_id=(d, k), device_id_type=MESH)

        def drain(ref, sem):
            pltpu.make_async_copy(ref, ref, sem).wait()

        def turn(first, second, dst):
            for n, ref in enumerate((first, second)):
                full = jnp.transpose(ref[...])
                for j in range(nh):
                    for h in range(HEADS):
                        row = j * width + h * dim
                        dst[j, h, n * dim : (n + 1) * dim, :] = full[row : row + dim, :]

        def to_head(src, dst, ssem, rsem, i):
            return remote(src.at[peer(i)], dst.at[k], ssem, rsem, (c, peer(i)))

        def kv_head(h, i):
            return remote(
                tkv.at[peer(i), h], kv[h].at[k], s_kv, r_kv.at[h, i], (c, peer(i))
            )

        turn(k_in, v_in, tkv)
        pl.semaphore_wait(barrier, nh - 1 + len(near))
        for h in range(HEADS):

            @pl.loop(1, nh)
            def _(i):
                kv_head(h, i).start()

        for h in range(HEADS):
            kv[h][k] = tkv[k, h]

        step = (1, -1)
        far = ((0, 1), (2, 3))

        def origin(i):
            return (k + nh - i) % nh

        def forward(h, s, stage, i):
            a1, a2, a3, a4, t3 = hops[h][s]
            src, dst = (
                (kv[h].at[origin(i)], a1.at[origin(i)]),
                (a1.at[origin(i)], a2.at[origin(i)]),
                (t3.at[pl.ds(4, 2)], a3.at[pl.ds(4, 2)]),
                (t3.at[pl.ds(0, 4)], a3.at[pl.ds(0, 4)]),
                (a3.at[pl.ds(4, 2)], a4),
            )[stage]
            rsem = r_f.at[h, s, i] if stage == 0 else r_h.at[h, s, stage - 1]
            return remote(src, dst, s_f.at[h, s], rsem, (at(0, step[s]), k))

        def across(h, src, ox, oz):
            o = ox * nz + oz
            return remote(src, flat[h][0].at[o], s_x.at[h], r_x.at[h], (at(ox, 0), k))

        def deliver(h, s, dist):
            arr, xs = flat[h][:2]
            oz = (step[s] * dist) % nz
            src = at(0, -step[s] * dist)
            buf = hops[h][s][dist - 1]
            if dist <= 2:
                for ox in range(1, nx):
                    xs[ox * nz + oz] = buf[pick(src, at(ox, 0))]
                    across(h, xs.at[ox * nz + oz], ox, oz).start()
                arr[oz] = buf[pick(src, c)]
            else:
                for n, ox in enumerate(range(nx) if dist == 3 else far[s]):
                    if ox == 0:
                        arr[oz] = buf[n]
                    else:
                        across(h, buf.at[n], ox, oz).start()

        def hop_one(h, first, last):
            @pl.loop(first, last)
            def _(i):
                kv_head(h, i).wait_recv()
                for s in range(2):
                    forward(h, s, 0, i).start()

        def hop_own(h):
            for s in range(2):
                forward(h, s, 0, 0).start()

        def row(h):
            for ox in range(1, nx):
                flat[h][1][ox * nz] = kv[h][pick(c, at(ox, 0))]
                across(h, flat[h][1].at[ox * nz], ox, 0).start()

        def hop_two(h):
            @pl.loop(0, nh)
            def _(i):
                for s in range(2):
                    forward(h, s, 0, i).wait_recv()
                    forward(h, s, 1, i).start()

            for s in range(2):
                deliver(h, s, 1)

        def hop_three(h):
            for s in range(2):

                a2, t3 = hops[h][s][1], hops[h][s][4]
                drain(a2, r_h.at[h, s, 0])
                src = at(0, -2 * step[s])
                for n, ox in enumerate(far[s]):
                    t3[nx + n] = a2[pick(src, at(ox, 2 * step[s]))]
                forward(h, s, 2, 0).start()
                for ox in range(nx):
                    t3[ox] = a2[pick(src, at(ox, step[s]))]
                forward(h, s, 3, 0).start()
            for s in range(2):
                deliver(h, s, 2)

        def hop_four(h):
            for s in range(2):
                forward(h, s, 2, 0).wait_recv()
                forward(h, s, 4, 0).start()
            for s in range(2):
                forward(h, s, 3, 0).wait_recv()
                deliver(h, s, 3)

        def hop_last(h):
            for s in range(2):
                forward(h, s, 4, 0).wait_recv()
                deliver(h, s, 4)

        hop_own(0)
        turn(q_in, g_in, tqd)
        hop_one(0, 1, nh)

        @pl.loop(1, nh)
        def _(i):
            to_head(tqd, qd, s_qd, r_qd, i).start()

        qd[k] = tqd[k]
        row(0)
        hop_two(0)
        hop_own(1)
        hop_one(1, 1, 4)
        hop_three(0)
        hop_one(1, 4, nh)
        row(1)
        hop_four(0)
        hop_two(1)
        hop_last(0)

        drain(qd.at[pl.ds(0, nh - 1)], r_qd)

        gacc[...] = jnp.zeros_like(gacc)

        def attend(b, h):
            arr, g = flat[h][0], flat[h][2]
            gain_h = gain[h]
            qt = qd[b, h, 0:dim, :] * factor
            dot = qd[b, h, dim:pair, :]
            q = jnp.transpose(qt)
            do = jnp.transpose(dot)
            sets = [kv[h][b]]
            for m in range(NEI):
                owner = nbr[b * NEI + m] // blocks
                ox = (x + nx - owner // nz) % nx
                oz = (z + nz - owner % nz) % nz
                sets.append(arr[ox * nz + oz])
            bias = [table[bidx[b * (NEI + 1) + m]] for m in range(NEI + 1)]
            scores = [mm(q, t[0:dim], 1, 0) + gain_h * e for t, e in zip(sets, bias)]
            top = jnp.max(scores[0], axis=1, keepdims=True)
            for s in scores[1:]:
                top = jnp.maximum(top, jnp.max(s, axis=1, keepdims=True))
            weights = [jnp.exp(s - top) for s in scores]
            total = sum(jnp.sum(w, axis=1, keepdims=True) for w in weights)
            inverse = 1.0 / total
            weights = [w * inverse for w in weights]
            wgrad = [mm(do, t[dim:pair], 1, 0) for t in sets]
            delta = sum(jnp.sum(w * d, axis=1, keepdims=True) for w, d in zip(weights, wgrad))
            sgrad = [w * (d - delta) for w, d in zip(weights, wgrad)]
            oq[b, h, 0:dim, :] = sum(mm(t[dim:pair], w, 1, 1) for t, w in zip(sets, weights))
            oq[b, h, dim:pair, :] = factor * sum(mm(t[0:dim], s, 1, 1) for t, s in zip(sets, sgrad))
            part = jnp.zeros((8, BLOCK), jnp.float32)
            for m in range(NEI + 1):
                dk = mm(qt, sgrad[m], 1, 0)
                dv = mm(dot, weights[m], 1, 0)
                if m == 0:
                    loc[b, h, 0:dim, :] = dk
                    loc[b, h, dim:pair, :] = dv
                else:
                    g[b * NEI + m - 1, 0:dim, :] = dk
                    g[b * NEI + m - 1, dim:pair, :] = dv
                scaled = gain_h * sgrad[m]
                if h == 0:
                    ds[b * (NEI + 1) + m] = scaled
                else:
                    ds[b * (NEI + 1) + m] += scaled
                prod = sgrad[m] * bias[m]
                part = part + jnp.sum(prod.reshape(BLOCK // 8, 8, BLOCK), axis=0)
            gacc[h] += part

        def compute(h, first, last):
            @pl.loop(first, last)
            def _(b):
                attend(b, h)

        def arrived(h):
            drain(flat[h][0].at[pl.ds(nz, nc - nz)], r_x.at[h])

        def send_oq(h, i):
            return remote(
                oq.at[peer(i), h], oqin.at[k, h], s_oq, r_oq, (c, peer(i))
            )

        def send_dkv(h, i):
            return remote(
                loc.at[peer(i), h], dkvin.at[k, h], s_dkv, r_dkv, (c, peer(i))
            )

        def aside(h, ox, oz):
            rs, xb = flat[h][3:5]
            return remote(rs.at[oz, ox], xb.at[oz, ox], s_y.at[h], r_y.at[h, oz], (at(-ox, 0), k))

        def gathered(h, oz):
            drain(flat[h][4].at[oz, pl.ds(1, nx - 1)], r_y.at[h, oz])

        def outputs(h):
            g, rs, xb = flat[h][2:5]
            for oz in (4, 3, 5, 2, 6, 1, 7, 0):
                for ox in range(1, nx):
                    rs[oz, ox] = g[rof[at(-ox, -oz)]]
                    aside(h, ox, oz).start()
                if oz > 0:
                    xb[oz, 0] = g[rof[at(0, -oz)]]

            @pl.loop(1, nh)
            def _(i):
                send_oq(h, i).start()

            oqin[k, h] = oq[k, h]

        def toward(s, dist):
            return (-step[s] * dist) % nz

        def back(h, s, stage, b):
            b4, b3, b2, b1, m2, m1 = backs[h][s]
            xb = flat[h][4]
            first = far[1 - s][0]
            src, dst = (
                (xb.at[4, pl.ds(first, 2)], b4),
                (xb.at[toward(s, 3)], b3.at[pl.ds(0, 4)]),
                (b4, b3.at[pl.ds(4, 2)]),
                (m2.at[b], b2.at[b]),
                (m1.at[b], b1.at[b]),
            )[stage]
            rsem = r_g.at[h, s, stage] if stage < 3 else r_b.at[h, s, stage - 3, b]
            return remote(src, dst, s_g.at[h, s], rsem, (at(0, step[s]), k))

        def back_start(h):
            gathered(h, 4)
            for s in range(2):
                back(h, s, 0, 0).start()
            for s in range(2):
                gathered(h, toward(s, 3))
                back(h, s, 1, 0).start()
            for s in range(2):
                back(h, s, 0, 0).wait_recv()
                back(h, s, 2, 0).start()

        def back_two(h):
            xb = flat[h][4]
            for s in range(2):
                gathered(h, toward(s, 2))
                back(h, s, 1, 0).wait_recv()
                back(h, s, 2, 0).wait_recv()

            @pl.loop(1, nh + 1)
            def _(i):
                b = peer(i)
                for s in range(2):
                    b3, m2 = backs[h][s][1], backs[h][s][4]
                    oz = toward(s, 2)
                    src = at(0, 2 * step[s])
                    acc = jnp.zeros((pair, BLOCK), jnp.float32)
                    for ox in range(nx):
                        acc = acc + xb[oz, ox] * is_block(src, at(ox, 0), b)
                        acc = acc + b3[ox] * is_block(src, at(ox, -step[s]), b)
                    for n, ox in enumerate(far[1 - s]):
                        acc = acc + b3[4 + n] * is_block(src, at(ox, -2 * step[s]), b)
                    m2[b] = acc
                    back(h, s, 3, b).start()

        def back_one(h):
            xb = flat[h][4]
            for s in range(2):
                gathered(h, toward(s, 1))

            @pl.loop(1, nh + 1)
            def _(i):
                b = peer(i)
                for s in range(2):
                    b2, m1 = backs[h][s][2], backs[h][s][5]
                    oz = toward(s, 1)
                    src = at(0, step[s])
                    back(h, s, 3, b).wait_recv()
                    acc = b2[b]
                    for ox in range(nx):
                        acc = acc + xb[oz, ox] * is_block(src, at(ox, 0), b)
                    m1[b] = acc
                    back(h, s, 4, b).start()

        def back_done(h):
            xb = flat[h][4]
            gathered(h, 0)

            def total(b):
                for s in range(2):
                    back(h, s, 4, b).wait_recv()
                acc = loc[b, h] + backs[h][0][3][b] + backs[h][1][3][b]
                for ox in range(1, nx):
                    acc = acc + xb[0, ox] * is_block(c, at(ox, 0), b)
                return acc

            @pl.loop(1, nh)
            def _(i):
                loc[peer(i), h] = total(peer(i))
                send_dkv(h, i).start()

            dkvin[k, h] = total(k)

        def table_head(i):
            return remote(
                tl.at[pl.ds(peer(i) * share, share)], trs.at[k], s_ta, r_ta, (c, peer(i))
            )

        def table_ctx(o):
            d = at(o // nz, o % nz)
            return remote(tb.at[d], tbin.at[c], s_tb, r_tb, (d, k))

        def table_gather(o):
            d = at(o // nz, o % nz)
            return remote(tc.at[c], tc.at[c], s_tc, r_tc, (d, k))

        def table_spread(i):
            return remote(
                tsum, table_out.at[pl.ds(k * share, share)], s_td, r_td, (c, peer(i))
            )

        per = BLOCK // piece

        def table_first():
            @pl.loop(0, nbias)
            def _(t):
                acc = jnp.zeros((BLOCK, BLOCK), jnp.float32)
                for r in range(blocks * (NEI + 1)):
                    acc = acc + ds[r] * (bidx[r] == t).astype(jnp.float32)
                tl[t] = acc

            @pl.loop(1, nh)
            def _(i):
                table_head(i).start()

            trs[k] = tl[pl.ds(k * share, share)]

        def table_second():
            drain(trs.at[pl.ds(0, nh - 1)], r_ta)

            mine = jnp.concatenate(
                [jnp.sum(gacc[h], axis=0, keepdims=True) for h in range(HEADS)]
                + [jnp.zeros((8 - HEADS, BLOCK), jnp.float32)],
                axis=0,
            )

            @pl.loop(0, share)
            def _(t):
                acc = trs[0, t]
                for i in range(1, nh):
                    acc = acc + trs[i, t]
                tsum[t] = acc

            @pl.loop(0, nc)
            def _(d):
                tb[d, 0:piece, :] = tsum[
                    d // per, pl.ds(pl.multiple_of((d % per) * piece, 8), piece), :
                ]
                tb[d, piece : piece + 8, :] = mine

            @pl.loop(1, nc)
            def _(o):
                table_ctx(o).start()

            tbin[c] = tb[c]

        def table_third():
            drain(tbin.at[pl.ds(0, nc - 1)], r_tb)

            acc = tbin[0]
            for i in range(1, nc):
                acc = acc + tbin[i]
            tc[c] = acc[0:piece]
            gain_out[...] = jnp.broadcast_to(
                jnp.sum(acc[piece : piece + 8], axis=1, keepdims=True), (8, BLOCK)
            )

            @pl.loop(1, nc)
            def _(o):
                table_gather(o).start()

        def table_fourth():
            drain(tc.at[pl.ds(0, nc - 1)], r_tc)

            @pl.loop(0, nc)
            def _(d):
                tsum[d // per, pl.ds(pl.multiple_of((d % per) * piece, 8), piece), :] = tc[d]

            @pl.loop(1, nh)
            def _(i):
                table_spread(i).start()

            table_out[pl.ds(k * share, share)] = tsum[...]

        def restore(src, first, second):
            for n, ref in enumerate((first, second)):
                rows = []
                for j in range(nh):
                    for h in range(HEADS):
                        rows.append(src[j, h, n * dim : (n + 1) * dim, :])
                ref[...] = jnp.transpose(jnp.concatenate(rows, axis=0))

        arrived(0)
        compute(0, 0, 3)
        hop_three(1)
        compute(0, 3, 6)
        hop_four(1)
        compute(0, 6, blocks)
        hop_last(1)
        outputs(0)
        arrived(1)
        compute(1, 0, 2)
        back_start(0)
        compute(1, 2, 4)
        back_two(0)
        compute(1, 4, 7)
        back_one(0)
        compute(1, 7, blocks)
        outputs(1)
        back_start(1)
        table_first()
        back_two(1)
        table_second()
        back_done(0)
        back_one(1)
        table_third()
        drain(oqin.at[pl.ds(0, nh - 1)], r_oq)
        restore(oqin, o_out, dq_out)
        table_fourth()
        back_done(1)
        drain(dkvin.at[pl.ds(0, nh - 1)], r_dkv)
        restore(dkvin, dk_out, dv_out)
        drain(table_out.at[pl.ds(0, nbias - share)], r_td)
        for sem in (s_kv, s_qd, s_oq, s_dkv):
            drain(oqin.at[pl.ds(0, nh - 1)], sem)
        for sem in (s_ta, s_td):
            drain(trs.at[pl.ds(0, nh - 1)], sem)
        drain(tbin.at[pl.ds(0, nc - 1)], s_tb)
        drain(tc.at[pl.ds(0, nc - 1)], s_tc)
        for h in range(HEADS):
            for sem in (s_x.at[h], s_y.at[h], s_f.at[h, 0], s_f.at[h, 1], s_g.at[h, 0], s_g.at[h, 1]):
                drain(flat[h][0].at[pl.ds(0, 3 * nz)], sem)

    def f32(*shape):
        return pltpu.VMEM(shape, jnp.float32)

    def sems(*shape):
        return pltpu.SemaphoreType.DMA(shape)

    one = pltpu.SemaphoreType.DMA
    scratch = (
        [f32(nh, HEADS, pair, BLOCK)] * 2
        + [f32(nh, pair, BLOCK)] * 2
        + [f32(nh, HEADS, pair, BLOCK)] * 5
        + [f32(blocks * (NEI + 1), BLOCK, BLOCK), f32(HEADS, 8, BLOCK)]
        + [f32(nbias, BLOCK, BLOCK), f32(nh, share, BLOCK, BLOCK), f32(share, BLOCK, BLOCK)]
        + [f32(nc, piece + 8, BLOCK)] * 2
        + [f32(nc, piece, BLOCK)]
        + [one, sems(HEADS, nh)]
        + [one] * 14
        + [sems(HEADS, 2), sems(HEADS, 2, nh), sems(HEADS, 2, 4)]
        + [sems(HEADS)] * 2
        + [sems(HEADS, 2), sems(HEADS, 2, 3), sems(HEADS, 2, 2, nh)]
        + [sems(HEADS), sems(HEADS, nz)]
        + [f32(n, pair, BLOCK) for n in (blocks, blocks, 6, 2, 6)] * (2 * HEADS)
        + [f32(n, pair, BLOCK) for n in (2, 6, blocks, blocks, blocks, blocks)] * (2 * HEADS)
        + [
            f32(nc, pair, BLOCK),
            f32(nc, pair, BLOCK),
            f32(requests, pair, BLOCK),
            f32(nz, nx, pair, BLOCK),
            f32(nz, nx, pair, BLOCK),
        ]
        * HEADS
    )
    return kernel, scratch


def solution(mesh):
    nc = mesh.shape["ctx"]
    nh = mesh.shape["head"]
    nx = 4
    nz = nc // nx

    def body(queries, keys, values, grad_out, neighbours, bias_index, bias_table, head_gain):
        rows, columns = queries.shape
        nbias = bias_table.shape[0]
        dim = columns // (nh * HEADS)
        blocks = nh
        requests = blocks * NEI
        me = lax.axis_index("ctx")
        asks = neighbours.reshape(nc, requests)
        owner = asks // blocks
        local = asks % blocks
        match = owner[None, :, :] == jnp.arange(nc)[:, None, None]
        key = jnp.max(jnp.where(match, local[None, :, :], -1), axis=2)
        own = lax.dynamic_index_in_dim(asks, me, 0, keepdims=False)
        wanted = (own // blocks)[None, :] == jnp.arange(nc)[:, None]
        rof = jnp.max(jnp.where(wanted, jnp.arange(requests)[None, :], 0), axis=1)
        kernel, scratch = make_kernel(nx, nz, nh, nbias, dim)
        smem = pl.BlockSpec(memory_space=pltpu.SMEM)
        vmem = pl.BlockSpec(memory_space=pltpu.VMEM)
        wide = jax.ShapeDtypeStruct((rows, columns), jnp.float32)
        outs = pl.pallas_call(
            kernel,
            out_shape=[wide] * 4
            + [
                jax.ShapeDtypeStruct(bias_table.shape, jnp.float32),
                jax.ShapeDtypeStruct((8, BLOCK), jnp.float32),
            ],
            in_specs=[smem] * 5 + [vmem] * 5,
            out_specs=[vmem] * 6,
            scratch_shapes=scratch,
            compiler_params=pltpu.CompilerParams(
                collective_id=0, has_side_effects=True, vmem_limit_bytes=60 * 1024 * 1024
            ),
        )(
            key.reshape(-1), rof, own, bias_index.reshape(-1), head_gain,
            queries, keys, values, grad_out, bias_table,
        )
        return (*outs[:5], outs[5][:HEADS, 0])

    return jax.shard_map(
        body,
        mesh=mesh,
        in_specs=(
            P(("ctx", "head"), None),
            P(("ctx", "head"), None),
            P(("ctx", "head"), None),
            P(("ctx", "head"), None),
            P(),
            P("ctx", None),
            P(),
            P("head"),
        ),
        out_specs=(
            P(("ctx", "head"), None),
            P(("ctx", "head"), None),
            P(("ctx", "head"), None),
            P(("ctx", "head"), None),
            P(),
            P("head"),
        ),
        check_vma=False,
    )
```

time: 208 us -> 182 us (0.88)
  Pallas kernels: 195 us -> 170 us
    pallas_call x1, Pallas kernels: 195 us -> 170 us  [body(): pl.pallas_call(kernel, out_shape=[wide] * 4 + [jax.ShapeDtypeStruct(bias_...]
where the time goes in v2:
time: 182 us
  Pallas kernels  170 us (93%)
  local copies, waits for them, and re-layouts  9.22 us (5%)
    pallas_call x1, Pallas kernels, body(): pl.pallas_call(kernel, out_shape=[wide] * 4 + [jax.ShapeDtypeStruct(bias_...  170 us
    unnamed x19, local copies, waits for them, and re-layouts  6.42 us

profile of v2, /device:TPU:1, one launch (start us, length us, event | category | flops | bytes accessed | tf_op | source)
XLA Modules:
  0.0 181.6 jit_solution(16977509108473947386)
XLA Ops:
  0.6 0.0 copy-start.5
  0.6 0.7 copy-done.5
  1.3 0.1 copy.20
  1.4 0.0 copy-start.4
  1.4 0.6 reshape.72.bidx
  2.0 0.1 copy-done.4
  2.1 0.1 copy.17
  2.2 0.1 reshape.70
  2.3 0.5 fusion.3
  2.9 0.6 select_reduce_fusion.1.rof
  3.5 0.1 copy.18
  3.6 0.1 copy.19
  3.6 0.1 select_reduce_fusion
  3.7 0.7 reshape.71.key
  4.4 170.4 %shard_map.127 = (f32[128,768]{1,0:T(8,128)}, f32[128,768]{1,0:T(8,128)}, f32[128,768]{1,0:T(8,128)}, f32[128,768]{1,0:T(8,128)}, f32[16,128,128]{2,1,0:T(8,128)}, /*index=5*/f32[8,128]{1,0:T(8,128)}) custom-call(s32[1024]{0:T(1024)} %reshape.71.key, s32[32]{0:T(128)} %select_reduce_fusion.1.rof, s32[16]{0:T(128)} %get-tuple-element.18.nbr, ...), custom_call_target="tpu_custom_call" | custom-call | tf_op jit(solution)/shard_map/pallas_call | solution.py:606
  174.8 1.3 slice_reduce_fusion
  176.1 0.0 copy-start.3
  176.1 0.0 copy-start.2
  176.1 1.8 %copy.26 = f32[128,768]{1,0:T(8,128)} copy(f32[128,768]{1,0:T(8,128)} %get-tuple-element.28) | data formatting | bytes 786432
  178.0 0.0 copy-done.3
  178.0 0.0 copy-start
  178.0 0.7 copy.27
  178.7 0.0 copy-done.2
  178.7 0.0 copy-start.1
  178.7 0.7 copy.28
  179.5 0.4 copy-done.1
  179.9 0.7 copy.29
  180.6 0.0 copy-done
  180.6 1.0 copy.30
  (1 shorter events, 0.0 us)
Async XLA Ops:
  0.6 0.7 copy-start.5
  1.4 0.7 copy-start.4
  176.1 1.8 %copy-start.3 = (f32[128,768]{1,0:T(8,128)S(1)}, f32[128,768]{1,0:T(8,128)}, u32[]{:S(2)}) copy-start(f32[128,768]{1,0:T(8,128)} %get-tuple-element.29) | copy-start | bytes 1179652
  176.1 2.6 %copy-start.2 = (f32[128,768]{1,0:T(8,128)S(1)}, f32[128,768]{1,0:T(8,128)}, u32[]{:S(2)}) copy-start(f32[128,768]{1,0:T(8,128)} %get-tuple-element.30) | copy-start | bytes 1179652
  178.0 2.6 %copy-start = (f32[16,128,128]{2,1,0:T(8,128)S(1)}, f32[16,128,128]{2,1,0:T(8,128)}, u32[]{:S(2)}) copy-start(f32[16,128,128]{2,1,0:T(8,128)} %get-tuple-element.32) | copy-start | bytes 3145732
  178.7 1.1 copy-start.1

commit v3 on v2

--- a/solution.py
+++ b/solution.py
@@ -26,6 +26,7 @@
     width = HEADS * dim
     share = nbias // nh
     piece = share * BLOCK // nc
+    quarter = share * BLOCK // nx
     factor = dim ** (-0.5)
 
     def kernel(
@@ -33,9 +34,9 @@
         q_in, k_in, v_in, g_in, table,
         o_out, dq_out, dk_out, dv_out, table_out, gain_out,
         tkv, tqd, kv0, kv1, qd, loc, oq, oqin, dkvin,
-        ds, gacc, tl, trs, tsum, tb, tbin, tc,
+        ds, gacc, tl, trs, tsum, tx, txin, tb, tbin, tc, tg,
         s_kv, r_kv, s_qd, r_qd, s_oq, r_oq, s_dkv, r_dkv,
-        s_ta, r_ta, s_tb, r_tb, s_tc, r_tc, s_td, r_td,
+        s_ta, r_ta, s_tx, r_tx, s_tb, r_tb, s_tc, r_tc, s_tg, r_tg, s_td, r_tm, r_td,
         s_f, r_f, r_h, s_x, r_x, s_g, r_g, r_b, s_y, r_y,
         *rest,
     ):
@@ -365,12 +366,13 @@
                     m2[b] = acc
                     back(h, s, 3, b).start()
 
-        def back_one(h):
+        def back_one(h, first=1, last=nh + 1):
             xb = flat[h][4]
-            for s in range(2):
-                gathered(h, toward(s, 1))
-
-            @pl.loop(1, nh + 1)
+            if first == 1:
+                for s in range(2):
+                    gathered(h, toward(s, 1))
+
+            @pl.loop(first, last)
             def _(i):
                 b = peer(i)
                 for s in range(2):
@@ -408,20 +410,26 @@
                 tl.at[pl.ds(peer(i) * share, share)], trs.at[k], s_ta, r_ta, (c, peer(i))
             )
 
-        def table_ctx(o):
-            d = at(o // nz, o % nz)
-            return remote(tb.at[d], tbin.at[c], s_tb, r_tb, (d, k))
-
-        def table_gather(o):
-            d = at(o // nz, o % nz)
-            return remote(tc.at[c], tc.at[c], s_tc, r_tc, (d, k))
-
-        def table_spread(i):
-            return remote(
-                tsum, table_out.at[pl.ds(k * share, share)], s_td, r_td, (c, peer(i))
-            )
-
-        per = BLOCK // piece
+        def table_x(ox):
+            return remote(tx.at[(x + ox) % nx], txin.at[x], s_tx, r_tx, (at(ox, 0), k))
+
+        def table_z(oz):
+            return remote(tb.at[(z + oz) % nz], tbin.at[z], s_tb, r_tb, (at(0, oz), k))
+
+        def gather_z(oz):
+            return remote(tc.at[z], tc.at[z], s_tc, r_tc, (at(0, oz), k))
+
+        def gather_x(ox):
+            return remote(tg.at[x], tg.at[x], s_tg, r_tg, (at(ox, 0), k))
+
+        mate = 2 * (k // 2) + 1 - k % 2
+
+        def table_y(i):
+            part = table_out.at[pl.ds(k * share, share)]
+            return remote(tsum, part, s_td, r_td.at[i], (c, (k + 2 * i) % nh))
+
+        def table_mate(src, j):
+            return remote(src, table_out.at[pl.ds(j * share, share)], s_td, r_tm, (c, mate))
 
         def table_first():
             @pl.loop(0, nbias)
@@ -438,61 +446,68 @@
             trs[k] = tl[pl.ds(k * share, share)]
 
         def table_second():
-            drain(trs.at[pl.ds(0, nh - 1)], r_ta)
-
             mine = jnp.concatenate(
                 [jnp.sum(gacc[h], axis=0, keepdims=True) for h in range(HEADS)]
                 + [jnp.zeros((8 - HEADS, BLOCK), jnp.float32)],
                 axis=0,
             )
-
-            @pl.loop(0, share)
-            def _(t):
-                acc = trs[0, t]
+            drain(trs.at[pl.ds(0, nh - 1)], r_ta)
+            for t in range(nx):
+                rows = pl.ds(t * quarter % BLOCK, quarter)
+                acc = trs[0, t * quarter // BLOCK, rows, :]
                 for i in range(1, nh):
-                    acc = acc + trs[i, t]
-                tsum[t] = acc
-
-            @pl.loop(0, nc)
-            def _(d):
-                tb[d, 0:piece, :] = tsum[
-                    d // per, pl.ds(pl.multiple_of((d % per) * piece, 8), piece), :
-                ]
-                tb[d, piece : piece + 8, :] = mine
-
-            @pl.loop(1, nc)
-            def _(o):
-                table_ctx(o).start()
-
-            tbin[c] = tb[c]
+                    acc = acc + trs[i, t * quarter // BLOCK, rows, :]
+                tx[t, 0:quarter, :] = acc
+                tx[t, quarter : quarter + 8, :] = mine
+            for ox in range(1, nx):
+                table_x(ox).start()
+            txin[x] = tx[x]
 
         def table_third():
-            drain(tbin.at[pl.ds(0, nc - 1)], r_tb)
-
+            drain(txin.at[pl.ds(0, nx - 1)], r_tx)
+            acc = txin[0]
+            for i in range(1, nx):
+                acc = acc + txin[i]
+            for t in range(nz):
+                tb[t, 0:piece, :] = acc[t * piece : (t + 1) * piece]
+                tb[t, piece : piece + 8, :] = acc[quarter:]
+            for oz in range(1, nz):
+                table_z(oz).start()
+            tbin[z] = tb[z]
+
+        def table_fourth():
+            drain(tbin.at[pl.ds(0, nz - 1)], r_tb)
             acc = tbin[0]
-            for i in range(1, nc):
+            for i in range(1, nz):
                 acc = acc + tbin[i]
-            tc[c] = acc[0:piece]
+            tc[z] = acc[0:piece]
             gain_out[...] = jnp.broadcast_to(
                 jnp.sum(acc[piece : piece + 8], axis=1, keepdims=True), (8, BLOCK)
             )
-
-            @pl.loop(1, nc)
-            def _(o):
-                table_gather(o).start()
-
-        def table_fourth():
-            drain(tc.at[pl.ds(0, nc - 1)], r_tc)
-
-            @pl.loop(0, nc)
-            def _(d):
-                tsum[d // per, pl.ds(pl.multiple_of((d % per) * piece, 8), piece), :] = tc[d]
-
-            @pl.loop(1, nh)
-            def _(i):
-                table_spread(i).start()
-
+            for oz in range(1, nz):
+                gather_z(oz).start()
+
+        def table_fifth():
+            drain(tc.at[pl.ds(0, nz - 1)], r_tc)
+            tg[x] = tc[...].reshape(quarter, BLOCK)
+            for ox in range(1, nx):
+                gather_x(ox).start()
+
+        def table_sixth():
+            drain(tg.at[pl.ds(0, nx - 1)], r_tg)
+            for t in range(nx):
+                tsum[t * quarter // BLOCK, pl.ds(t * quarter % BLOCK, quarter), :] = tg[t]
+            for i in range(1, nh // 2):
+                table_y(i).start()
+            table_mate(tsum, k).start()
             table_out[pl.ds(k * share, share)] = tsum[...]
+
+        def table_last():
+            for i in range(1, nh // 2):
+                j = (k + nh - 2 * i) % nh
+                part = table_out.at[pl.ds(j * share, share)]
+                drain(part, r_td.at[i])
+                table_mate(part, j).start()
 
         def restore(src, first, second):
             for n, ref in enumerate((first, second)):
@@ -519,26 +534,32 @@
         back_one(0)
         compute(1, 7, blocks)
         outputs(1)
+        table_first()
         back_start(1)
-        table_first()
+        back_done(0)
         back_two(1)
         table_second()
-        back_done(0)
-        back_one(1)
         table_third()
+        back_one(1, 1, 5)
+        table_fourth()
+        back_one(1, 5)
+        table_fifth()
+        table_sixth()
         drain(oqin.at[pl.ds(0, nh - 1)], r_oq)
         restore(oqin, o_out, dq_out)
-        table_fourth()
         back_done(1)
+        table_last()
         drain(dkvin.at[pl.ds(0, nh - 1)], r_dkv)
         restore(dkvin, dk_out, dv_out)
-        drain(table_out.at[pl.ds(0, nbias - share)], r_td)
+        drain(table_out.at[pl.ds(0, nbias // 2)], r_tm)
         for sem in (s_kv, s_qd, s_oq, s_dkv):
             drain(oqin.at[pl.ds(0, nh - 1)], sem)
         for sem in (s_ta, s_td):
             drain(trs.at[pl.ds(0, nh - 1)], sem)
-        drain(tbin.at[pl.ds(0, nc - 1)], s_tb)
-        drain(tc.at[pl.ds(0, nc - 1)], s_tc)
+        drain(txin.at[pl.ds(0, nx - 1)], s_tx)
+        drain(tbin.at[pl.ds(0, nz - 1)], s_tb)
+        drain(tc.at[pl.ds(0, nz - 1)], s_tc)
+        drain(tg.at[pl.ds(0, nx - 1)], s_tg)
         for h in range(HEADS):
             for sem in (s_x.at[h], s_y.at[h], s_f.at[h, 0], s_f.at[h, 1], s_g.at[h, 0], s_g.at[h, 1]):
                 drain(flat[h][0].at[pl.ds(0, 3 * nz)], sem)
@@ -556,10 +577,12 @@
         + [f32(nh, HEADS, pair, BLOCK)] * 5
         + [f32(blocks * (NEI + 1), BLOCK, BLOCK), f32(HEADS, 8, BLOCK)]
         + [f32(nbias, BLOCK, BLOCK), f32(nh, share, BLOCK, BLOCK), f32(share, BLOCK, BLOCK)]
-        + [f32(nc, piece + 8, BLOCK)] * 2
-        + [f32(nc, piece, BLOCK)]
+        + [f32(nx, quarter + 8, BLOCK)] * 2
+        + [f32(nz, piece + 8, BLOCK)] * 2
+        + [f32(nz, piece, BLOCK), f32(nx, quarter, BLOCK)]
         + [one, sems(HEADS, nh)]
-        + [one] * 14
+        + [one] * 18
+        + [sems(nh // 2)]
         + [sems(HEADS, 2), sems(HEADS, 2, nh), sems(HEADS, 2, 4)]
         + [sems(HEADS)] * 2
         + [sems(HEADS, 2), sems(HEADS, 2, 3), sems(HEADS, 2, 2, nh)]

time: 182 us -> 171 us (0.940)
  Pallas kernels: 170 us -> 159 us
    pallas_call x1, Pallas kernels: 170 us -> 159 us  [body(): pl.pallas_call(kernel, out_shape=[wide] * 4 + [jax.ShapeDtypeStruct(bias_...]
where the time goes in v3:
time: 171 us; the launch traced here: 170 us
  Pallas kernels  159 us (93%)
  local copies, waits for them, and re-layouts  9.22 us (5%)
    pallas_call x1, Pallas kernels, body(): pl.pallas_call(kernel, out_shape=[wide] * 4 + [jax.ShapeDtypeStruct(bias_...  159 us
    unnamed x19, local copies, waits for them, and re-layouts  6.42 us

profile of v3, /device:TPU:1, one launch (start us, length us, event | category | flops | bytes accessed | tf_op | source)
XLA Modules:
  0.0 170.3 jit_solution(18479093172152888)
XLA Ops:
  0.6 0.0 copy-start.5
  0.6 0.7 copy-done.5
  1.3 0.1 copy.20
  1.4 0.0 copy-start.4
  1.4 0.6 reshape.72.bidx
  2.0 0.1 copy-done.4
  2.1 0.1 copy.17
  2.2 0.1 reshape.70
  2.3 0.5 fusion.3
  2.9 0.6 select_reduce_fusion.1.rof
  3.5 0.1 copy.18
  3.6 0.1 copy.19
  3.6 0.1 select_reduce_fusion
  3.7 0.7 reshape.71.key
  4.4 159.1 %shard_map.127 = (f32[128,768]{1,0:T(8,128)}, f32[128,768]{1,0:T(8,128)}, f32[128,768]{1,0:T(8,128)}, f32[128,768]{1,0:T(8,128)}, f32[16,128,128]{2,1,0:T(8,128)}, /*index=5*/f32[8,128]{1,0:T(8,128)}) custom-call(s32[1024]{0:T(1024)} %reshape.71.key, s32[32]{0:T(128)} %select_reduce_fusion.1.rof, s32[16]{0:T(128)} %get-tuple-element.18.nbr, ...), custom_call_target="tpu_custom_call" | custom-call | tf_op jit(solution)/shard_map/pallas_call | solution.py:629
  163.5 1.3 slice_reduce_fusion
  164.9 0.0 copy-start.3
  164.9 0.0 copy-start.2
  164.9 1.8 %copy.26 = f32[128,768]{1,0:T(8,128)} copy(f32[128,768]{1,0:T(8,128)} %get-tuple-element.28) | data formatting | bytes 786432
  166.7 0.0 copy-done.3
  166.7 0.0 copy-start
  166.7 0.7 copy.27
  167.4 0.0 copy-done.2
  167.5 0.0 copy-start.1
  167.5 0.7 copy.28
  168.2 0.4 copy-done.1
  168.6 0.7 copy.29
  169.3 0.0 copy-done
  169.3 1.0 copy.30
  (1 shorter events, 0.0 us)
Async XLA Ops:
  0.6 0.7 copy-start.5
  1.4 0.7 copy-start.4
  164.9 1.8 %copy-start.3 = (f32[128,768]{1,0:T(8,128)S(1)}, f32[128,768]{1,0:T(8,128)}, u32[]{:S(2)}) copy-start(f32[128,768]{1,0:T(8,128)} %get-tuple-element.29) | copy-start | bytes 1179652
  164.9 2.6 %copy-start.2 = (f32[128,768]{1,0:T(8,128)S(1)}, f32[128,768]{1,0:T(8,128)}, u32[]{:S(2)}) copy-start(f32[128,768]{1,0:T(8,128)} %get-tuple-element.30) | copy-start | bytes 1179652
  166.7 2.6 %copy-start = (f32[16,128,128]{2,1,0:T(8,128)S(1)}, f32[16,128,128]{2,1,0:T(8,128)}, u32[]{:S(2)}) copy-start(f32[16,128,128]{2,1,0:T(8,128)} %get-tuple-element.32) | copy-start | bytes 3145732
  167.5 1.1 copy-start.1

commit v4 on v3

--- a/solution.py
+++ b/solution.py
@@ -31,8 +31,9 @@
 
     def kernel(
         key, rof, nbr, bidx, gain,
-        q_in, k_in, v_in, g_in, table,
+        q_hbm, k_hbm, v_hbm, g_hbm, table_hbm,
         o_out, dq_out, dk_out, dv_out, table_out, gain_out,
+        q_in, k_in, v_in, g_in, table, s_in,
         tkv, tqd, kv0, kv1, qd, loc, oq, oqin, dkvin,
         ds, gacc, tl, trs, tsum, tx, txin, tb, tbin, tc, tg,
         s_kv, r_kv, s_qd, r_qd, s_oq, r_oq, s_dkv, r_dkv,
@@ -72,6 +73,17 @@
                 src, dst, ssem, rsem, device_id=dev, device_id_type=MESH
             )
 
+        inputs = [
+            pltpu.make_async_copy(src, dst, s_in.at[n])
+            for n, (src, dst) in enumerate(
+                (
+                    (k_hbm, k_in), (v_hbm, v_in), (q_hbm, q_in), (g_hbm, g_in), (table_hbm, table)
+                )
+            )
+        ]
+        for copy in inputs:
+            copy.start()
+
         barrier = pltpu.get_barrier_semaphore()
 
         @pl.loop(1, nh)
@@ -101,6 +113,8 @@
                 tkv.at[peer(i), h], kv[h].at[k], s_kv, r_kv.at[h, i], (c, peer(i))
             )
 
+        inputs[0].wait()
+        inputs[1].wait()
         turn(k_in, v_in, tkv)
         pl.semaphore_wait(barrier, nh - 1 + len(near))
         for h in range(HEADS):
@@ -206,6 +220,8 @@
                 deliver(h, s, 4)
 
         hop_own(0)
+        inputs[2].wait()
+        inputs[3].wait()
         turn(q_in, g_in, tqd)
         hop_one(0, 1, nh)
 
@@ -227,6 +243,7 @@
 
         drain(qd.at[pl.ds(0, nh - 1)], r_qd)
 
+        inputs[4].wait()
         gacc[...] = jnp.zeros_like(gacc)
 
         def attend(b, h):
@@ -481,9 +498,7 @@
             for i in range(1, nz):
                 acc = acc + tbin[i]
             tc[z] = acc[0:piece]
-            gain_out[...] = jnp.broadcast_to(
-                jnp.sum(acc[piece : piece + 8], axis=1, keepdims=True), (8, BLOCK)
-            )
+            gain_out[...] = acc[piece : piece + 8]
             for oz in range(1, nz):
                 gather_z(oz).start()
 
@@ -572,7 +587,9 @@
 
     one = pltpu.SemaphoreType.DMA
     scratch = (
-        [f32(nh, HEADS, pair, BLOCK)] * 2
+        [f32(BLOCK, nh * width)] * 4
+        + [f32(nbias, BLOCK, BLOCK), sems(5)]
+        + [f32(nh, HEADS, pair, BLOCK)] * 2
         + [f32(nh, pair, BLOCK)] * 2
         + [f32(nh, HEADS, pair, BLOCK)] * 5
         + [f32(blocks * (NEI + 1), BLOCK, BLOCK), f32(HEADS, 8, BLOCK)]
@@ -633,17 +650,38 @@
                 jax.ShapeDtypeStruct(bias_table.shape, jnp.float32),
                 jax.ShapeDtypeStruct((8, BLOCK), jnp.float32),
             ],
-            in_specs=[smem] * 5 + [vmem] * 5,
+            in_specs=[smem] * 5 + [pl.BlockSpec(memory_space=pltpu.HBM)] * 5,
             out_specs=[vmem] * 6,
             scratch_shapes=scratch,
             compiler_params=pltpu.CompilerParams(
-                collective_id=0, has_side_effects=True, vmem_limit_bytes=60 * 1024 * 1024
+                collective_id=0, has_side_effects=True, vmem_limit_bytes=52 * 1024 * 1024
             ),
         )(
             key.reshape(-1), rof, own, bias_index.reshape(-1), head_gain,
             queries, keys, values, grad_out, bias_table,
         )
-        return (*outs[:5], outs[5][:HEADS, 0])
+        def store(*refs):
+            ins, dst, sem = refs[:6], refs[6:12], refs[12]
+            copies = [pltpu.make_async_copy(ins[n], dst[n], sem.at[n]) for n in range(5)]
+            for copy in copies:
+                copy.start()
+            for h in range(HEADS):
+                dst[5][h] = jnp.sum(ins[5][h : h + 1, :])
+            for copy in copies:
+                copy.wait()
+
+        return pl.pallas_call(
+            store,
+            out_shape=[wide] * 4
+            + [
+                jax.ShapeDtypeStruct(bias_table.shape, jnp.float32),
+                jax.ShapeDtypeStruct((HEADS,), jnp.float32),
+            ],
+            in_specs=[vmem] * 6,
+            out_specs=[pl.BlockSpec(memory_space=pl.ANY)] * 5 + [smem],
+            scratch_shapes=[pltpu.SemaphoreType.DMA((5,))],
+            compiler_params=pltpu.CompilerParams(vmem_limit_bytes=8 * 1024 * 1024),
+        )(*outs)
 
     return jax.shard_map(
         body,

time: 171 us -> 164 us (0.959)
  local copies, waits for them, and re-layouts: 9.22 us -> 3.8 us
    unnamed x19 -> x8, local copies, waits for them, and re-layouts: 6.42 us -> 3.41 us
    pallas_call x0 -> x1, Pallas kernels: none -> 2.05 us  [body(): pl.pallas_call(store, out_shape=[wide] * 4 + [jax.ShapeDtypeStruct(bias_t...]
    pallas_call x1, Pallas kernels: 159 us -> 157 us  [body(): pl.pallas_call(kernel, out_shape=[wide] * 4 + [jax.ShapeDtypeStruct(bias_...]
where the time goes in v4:
time: 164 us
  Pallas kernels  159 us (97%)
  local copies, waits for them, and re-layouts  3.8 us (2%)
    pallas_call x1, Pallas kernels, body(): pl.pallas_call(kernel, out_shape=[wide] * 4 + [jax.ShapeDtypeStruct(bias_...  157 us
    unnamed x8, local copies, waits for them, and re-layouts  3.41 us

profile of v4, /device:TPU:1, one launch (start us, length us, event | category | flops | bytes accessed | tf_op | source)
XLA Modules:
  0.0 163.9 jit_solution(16103466356703232357)
XLA Ops:
  0.6 0.0 copy-start.1
  0.6 0.8 copy.20
  1.5 0.1 reshape.72.bidx
  1.5 0.8 copy.17
  2.4 0.1 reshape.70
  2.5 0.1 select_reduce_fusion.1.rof
  2.6 0.1 copy.18
  2.7 0.1 copy.19
  2.8 0.1 select_reduce_fusion
  2.9 0.0 copy-start.2
  2.9 0.1 reshape.71.key
  2.9 0.0 copy-done.1
  2.9 0.6 copy-done.2
  3.5 157.1 %shard_map.127 = (f32[128,768]{1,0:T(8,128)S(1)}, f32[128,768]{1,0:T(8,128)S(1)}, f32[128,768]{1,0:T(8,128)S(1)}, f32[128,768]{1,0:T(8,128)S(1)}, f32[16,128,128]{2,1,0:T(8,128)}, /*index=5*/f32[8,128]{1,0:T(8,128)S(1)}) custom-call(s32[1024]{0:T(1024)S(1)} %reshape.71.key, s32[32]{0:T(128)S(1)} %select_reduce_fusion.1.rof, s32[16]{0:T(128)S(1)} %get-tuple-element.18.nbr, ...), custom_call_target="tpu_custom_call" | custom-call | tf_op jit(solution)/shard_map/pallas_call | solution.py:646
  160.7 0.0 copy-start
  160.7 1.2 copy-done
  161.9 2.0 %shard_map.128 = (f32[128,768]{1,0:T(8,128)}, f32[128,768]{1,0:T(8,128)}, f32[128,768]{1,0:T(8,128)}, f32[128,768]{1,0:T(8,128)}, f32[16,128,128]{2,1,0:T(8,128)}, /*index=5*/f32[2]{0:T(128)}) custom-call(f32[128,768]{1,0:T(8,128)S(1)} %get-tuple-element.12.refs_0_, f32[128,768]{1,0:T(8,128)S(1)} %get-tuple-element.13.refs_1_, ...), custom_call_target="tpu_custom_call" | custom-call | tf_op jit(solution)/shard_map/pallas_call | solution.py:673
  (2 shorter events, 0.0 us)
Async XLA Ops:
  0.6 2.3 %copy-start.1 = (f32[128,768]{1,0:T(8,128)S(1)}, f32[128,768]{1,0:T(8,128)}, u32[]{:S(2)}) copy-start(f32[128,768]{1,0:T(8,128)} %q_hbm.1) | copy-start | bytes 1179652
  2.9 0.7 copy-start.2
  160.7 1.2 copy-start

commit v5 on v4

--- a/solution.py
+++ b/solution.py
@@ -558,10 +558,10 @@
         back_one(1, 1, 5)
         table_fourth()
         back_one(1, 5)
+        drain(oqin.at[pl.ds(0, nh - 1)], r_oq)
+        restore(oqin, o_out, dq_out)
         table_fifth()
         table_sixth()
-        drain(oqin.at[pl.ds(0, nh - 1)], r_oq)
-        restore(oqin, o_out, dq_out)
         back_done(1)
         table_last()
         drain(dkvin.at[pl.ds(0, nh - 1)], r_dkv)

time: 164 us -> 164 us (level)
  no operation moved by 1% of the time
where the time goes in v5:
time: 164 us
  Pallas kernels  159 us (97%)
  local copies, waits for them, and re-layouts  3.8 us (2%)
    pallas_call x1, Pallas kernels, body(): pl.pallas_call(kernel, out_shape=[wide] * 4 + [jax.ShapeDtypeStruct(bias_...  157 us
    unnamed x8, local copies, waits for them, and re-layouts  3.41 us

profile of v5, /device:TPU:1, one launch (start us, length us, event | category | flops | bytes accessed | tf_op | source)
XLA Modules:
  0.0 163.9 jit_solution(8567510719846530236)
XLA Ops:
  0.6 0.0 copy-start.1
  0.6 0.8 copy.20
  1.5 0.1 reshape.72.bidx
  1.5 0.8 copy.17
  2.4 0.1 reshape.70
  2.5 0.1 select_reduce_fusion.1.rof
  2.6 0.1 copy.18
  2.7 0.1 copy.19
  2.8 0.1 select_reduce_fusion
  2.9 0.0 copy-start.2
  2.9 0.1 reshape.71.key
  2.9 0.0 copy-done.1
  2.9 0.6 copy-done.2
  3.5 157.1 %shard_map.127 = (f32[128,768]{1,0:T(8,128)S(1)}, f32[128,768]{1,0:T(8,128)S(1)}, f32[128,768]{1,0:T(8,128)S(1)}, f32[128,768]{1,0:T(8,128)S(1)}, f32[16,128,128]{2,1,0:T(8,128)}, /*index=5*/f32[8,128]{1,0:T(8,128)S(1)}) custom-call(s32[1024]{0:T(1024)S(1)} %reshape.71.key, s32[32]{0:T(128)S(1)} %select_reduce_fusion.1.rof, s32[16]{0:T(128)S(1)} %get-tuple-element.18.nbr, ...), custom_call_target="tpu_custom_call" | custom-call | tf_op jit(solution)/shard_map/pallas_call | solution.py:646
  160.7 0.0 copy-start
  160.7 1.2 copy-done
  161.9 2.0 %shard_map.128 = (f32[128,768]{1,0:T(8,128)}, f32[128,768]{1,0:T(8,128)}, f32[128,768]{1,0:T(8,128)}, f32[128,768]{1,0:T(8,128)}, f32[16,128,128]{2,1,0:T(8,128)}, /*index=5*/f32[2]{0:T(128)}) custom-call(f32[128,768]{1,0:T(8,128)S(1)} %get-tuple-element.12.refs_0_, f32[128,768]{1,0:T(8,128)S(1)} %get-tuple-element.13.refs_1_, ...), custom_call_target="tpu_custom_call" | custom-call | tf_op jit(solution)/shard_map/pallas_call | solution.py:673
  (2 shorter events, 0.0 us)
Async XLA Ops:
  0.6 2.3 %copy-start.1 = (f32[128,768]{1,0:T(8,128)S(1)}, f32[128,768]{1,0:T(8,128)}, u32[]{:S(2)}) copy-start(f32[128,768]{1,0:T(8,128)} %q_hbm.1) | copy-start | bytes 1179652
  2.9 0.7 copy-start.2
  160.7 1.2 copy-start
